TPU v7x, 256 devices: a whole 4x4x8 slice. The times are simulated.
256 devices in a mesh: dp: 16 (over z, core), tensor: 4 (over y), corpus: 4 (over x).
Axes of the slice: x: 4, y: 4, z: 8, core: 2. Of those that a mesh axis runs over, the one named last changes fastest.
Arguments:
- queries: bfloat16 [4096, 2048], P(('dp', 'tensor', 'corpus')), may hold values from -24 to 24
- passages: bfloat16 [65536, 2048], P(('dp', 'corpus'), 'tensor'), may hold values from -6 to 6
- pos_ids: int32 [4096], P(('dp', 'tensor', 'corpus')), may hold values from 0 to 65535, as said below
- neg_ids: int32 [4096, 32], P(('dp', 'tensor', 'corpus')), may hold values from 0 to 65535, as said below
Outputs:
- grad_query: float32 [4096, 2048], P(('dp', 'tensor', 'corpus'))
- losses: float32 [4096], P(('dp', 'tensor', 'corpus'))
- grad_pass: float32 [65536, 2048], P(('dp', 'corpus'), 'tensor')
Inputs may be any that keep to these rules, and one draw needn't show every extreme that they name: `pos_ids`: together with neg_ids: the ids named by the 16 queries of one device, positives and negatives together, fall at most 16 times into one block of 1024 passage rows (rows b * 1024 to (b + 1) * 1024 - 1), and exactly 16 times into one block that is the same for every device. Ids may repeat. `neg_ids`: counted together with pos_ids as stated there.
All inputs are finite; a program needn't handle non-finite values.
Results may differ from a plain program's by a relative error of at most 0.0035.
Values may be sent and summed in bfloat16 or wider, within the bound.
A program may use at most 128 MiB of HBM per device.

v0:
```python
import jax
import jax.numpy as jnp
from jax import lax
from jax.sharding import PartitionSpec as P


def lookup_rows(row_table, asked_ids):
    return jnp.take(row_table, asked_ids, axis=0, mode="fill", fill_value=0)


def body(queries, passages, pos_ids, neg_ids):
    per_device, feat_width = queries.shape
    block_rows, shard_width = passages.shape
    neg_count = neg_ids.shape[1]
    owners = lax.axis_size("dp") * lax.axis_size("corpus")
    slot_count = 2 * per_device * (neg_count + 1) // owners
    score_scale = feat_width ** (-0.5)
    wanted = jnp.concatenate([pos_ids[:, None], neg_ids], axis=1).reshape(-1)
    owner_of = wanted // block_rows
    local_row = wanted % block_rows
    matches = (owner_of[:, None] == jnp.arange(owners)[None, :]).astype(jnp.int32)
    earlier = jnp.cumsum(matches, axis=0) - matches
    slot_of = owner_of * slot_count + jnp.sum(earlier * matches, axis=1)
    send_ids = jnp.full((owners * slot_count,), block_rows, jnp.int32).at[slot_of].set(local_row)
    send_ids = send_ids.reshape(owners, slot_count)
    row_table = lax.all_gather(passages, "tensor", axis=1, tiled=True)
    asked_ids = lax.all_to_all(send_ids, ("dp", "corpus"), split_axis=0, concat_axis=0, tiled=True)
    found = lookup_rows(row_table, asked_ids)
    fetched = lax.all_to_all(found, ("dp", "corpus"), split_axis=0, concat_axis=0, tiled=True)
    gathered = fetched.reshape(owners * slot_count, feat_width)[slot_of]
    gathered = gathered.reshape(per_device, neg_count + 1, feat_width)
    pos_rows = gathered[:, 0, :]
    neg_rows = gathered[:, 1:, :]
    in_batch = lax.all_gather(pos_rows, "dp", axis=0, tiled=True)
    columns = in_batch.shape[0]
    in_scores = (
        lax.dot_general(
            queries, in_batch, (((1,), (1,)), ((), ())), preferred_element_type=jnp.float32
        )
        * score_scale
    )
    neg_scores = (
        jnp.einsum("md,mkd->mk", queries, neg_rows, preferred_element_type=jnp.float32)
        * score_scale
    )
    logits = jnp.concatenate([in_scores, neg_scores], axis=1)
    row_max = jnp.max(logits, axis=1, keepdims=True)
    exponent = jnp.exp(logits - row_max)
    denominator = jnp.sum(exponent, axis=1, keepdims=True)
    own_col = lax.axis_index("dp") * per_device + jnp.arange(per_device)
    target = (jnp.arange(columns + neg_count)[None, :] == own_col[:, None]).astype(jnp.float32)
    losses = jnp.log(denominator[:, 0]) + row_max[:, 0] - jnp.sum(target * logits, axis=1)
    weights = (exponent / denominator - target).astype(jnp.bfloat16)
    in_weights = weights[:, :columns]
    neg_weights = weights[:, columns:]
    grad_query = jnp.dot(in_weights, in_batch, preferred_element_type=jnp.float32)
    grad_query = grad_query + jnp.einsum(
        "mk,mkd->md", neg_weights, neg_rows, preferred_element_type=jnp.float32
    )
    grad_query = grad_query * score_scale
    in_terms = lax.dot_general(
        in_weights, queries, (((0,), (0,)), ((), ())), preferred_element_type=jnp.float32
    )
    pos_grad = lax.psum_scatter(in_terms, "dp", scatter_dimension=0, tiled=True) * score_scale
    neg_grad = (
        neg_weights.astype(jnp.float32)[:, :, None]
        * queries.astype(jnp.float32)[:, None, :]
        * score_scale
    )
    row_grads = jnp.concatenate([pos_grad[:, None, :], neg_grad], axis=1).astype(jnp.bfloat16)
    row_grads = row_grads.reshape(-1, feat_width)
    grad_slots = (
        jnp.zeros((owners * slot_count, feat_width), jnp.bfloat16).at[slot_of].set(row_grads)
    )
    grad_slots = grad_slots.reshape(owners, slot_count, feat_width)
    arrived = lax.all_to_all(grad_slots, ("dp", "corpus"), split_axis=0, concat_axis=0, tiled=True)
    accum_grad = jnp.zeros((block_rows, feat_width), jnp.float32)
    accum_grad = accum_grad.at[asked_ids.reshape(-1)].add(
        arrived.reshape(-1, feat_width).astype(jnp.float32), mode="drop"
    )
    grad_pass = lax.psum_scatter(accum_grad, "tensor", scatter_dimension=1, tiled=True)
    return (grad_query, losses, grad_pass)


def solution(mesh):
    in_specs = (
        P(("dp", "tensor", "corpus"), None),
        P(("dp", "corpus"), "tensor"),
        P(("dp", "tensor", "corpus")),
        P(("dp", "tensor", "corpus"), None),
    )
    out_specs = (
        P(("dp", "tensor", "corpus"), None),
        P(("dp", "tensor", "corpus")),
        P(("dp", "corpus"), "tensor"),
    )
    return jax.shard_map(body, mesh=mesh, in_specs=in_specs, out_specs=out_specs, check_vma=False)
```

profile of v0, /device:TPU:1, one launch (start us, length us, event | category | flops | bytes accessed | tf_op | source)
XLA Modules:
  0.0 520.4 jit_solution(17081883421997860384)
XLA Ops:
  7.2 0.0 all-gather.4.cloned.1.call-start
  7.2 0.7 all-gather.4.cloned.1.call-update
  7.9 0.7 copy.13
  8.6 0.8 pad_add_fusion
  9.4 0.1 reshape.217
  9.5 0.1 reshape.218
  9.7 1.5 reduce-window.6
  11.2 0.3 slice_reduce_fusion
  11.5 0.1 bitcast_bitcast_fusion
  11.7 4.1 scatter_custom_fusion
  15.8 0.1 all_to_all.16
  15.8 22.0 %all_to_all.25 = s32[64,1,16]{2,1,0:T(1,128)S(1)} all-to-all(s32[64,1,16]{2,1,0:T(1,128)S(1)} %bitcast.53), channel_id=1, replica_groups=mesh['dp'=16,'tensor'=4,'corpus'=4] {'dp','corpus'}, dimensions={0} | all-to-all | bytes 8192 | tf_op jit(solution)/shard_map/all_to_all | solution.py:27
  37.8 0.1 reshape.229
  37.9 26.3 %all-gather.4.cloned.1.call-done = bf16[1024,2048]{1,0:T(8,128)(2,1)} async-done(((bf16[1024,512]{1,0:T(8,128)(2,1)}), bf16[1024,2048]{1,0:T(8,128)(2,1)}) %all-gather.4.cloned.1.call-update) | async-done | bytes 4194320 | tf_op jit(solution)/shard_map/all_gather | solution.py:26
  64.2 11.6 %gather_fusion = bf16[1024,2048]{1,0:T(8,128)(2,1)} fusion(bf16[1024,2048]{1,0:T(8,128)(2,1)} %all-gather.4.cloned.1.call-done, s32[1024]{0:T(1024)S(1)} %broadcast_clamp_fusion), kind=kCustom, calls=%fused_computation | custom fusion | bytes 8392704 | tf_op jit(solution)/shard_map/jit(_take)/gather | solution.py:8
  75.8 4.5 broadcast_select_fusion
  80.3 11.0 %all-to-all-start.1 = ((bf16[64,16,2048]{2,1,0:T(8,128)(2,1)}), bf16[64,16,2048]{2,1,0:T(8,128)(2,1)}, u32[]{:S(2)}, u32[]{:S(2)}) async-start(bf16[64,16,2048]{2,1,0:T(8,128)(2,1)} %broadcast_select_fusion), calls=%async_computation.1 | async-start | bytes 8388608 | tf_op jit(solution)/shard_map/all_to_all | solution.py:29
  91.3 0.0 all-gather.6.cloned.1.call-start
  91.4 93.5 %all-to-all-done.1 = bf16[64,16,2048]{2,1,0:T(8,128)(2,1)} async-done(((bf16[64,16,2048]{2,1,0:T(8,128)(2,1)}), bf16[64,16,2048]{2,1,0:T(8,128)(2,1)}, u32[]{:S(2)}, u32[]{:S(2)}) %all-to-all-start.1) | async-done | bytes 4194336 | tf_op jit(solution)/shard_map/all_to_all | solution.py:29
  184.9 9.0 %gather_fusion.1 = bf16[528,2048]{1,0:T(8,128)(2,1)S(1)} fusion(bf16[1024,2048]{1,0:T(8,128)(2,1)} %bitcast.6, s32[1024]{0:T(1024)S(1)} %pad_clamp_fusion), kind=kCustom, calls=%fused_computation.1 | custom fusion | bytes 4327488 | tf_op jit(solution)/shard_map/gather | solution.py:30
  193.9 0.0 copy-start.1
  193.9 1.9 reshape.222
  195.8 1.1 slice.34
  196.9 0.7 copy.17
  197.6 0.0 all-gather.6.cloned.1.call-update
  197.6 0.2 reduce-scatter.3.cloned.1.call-start
  197.8 0.0 copy-done.1
  197.8 2.4 fusion.8
  200.2 0.1 fusion.26
  200.4 34.0 %all-gather.6.cloned.1.call-done = bf16[256,1,2048]{2,0,1:T(8,128)(2,1)} async-done(((bf16[16,1,2048]{2,0,1:T(8,128)(2,1)}), bf16[256,1,2048]{2,0,1:T(8,128)(2,1)}) %all-gather.6.cloned.1.call-update) | async-done | bytes 1048592 | tf_op jit(solution)/shard_map/all_gather | solution.py:34
  234.4 1.7 fusion.27
  236.1 0.2 select_reduce_fusion
  236.3 0.1 subtract_convert_fusion
  236.4 1.8 fusion.18
  238.2 0.0 reduce-scatter.3.cloned.1.call-update
  238.2 1.8 multiply_convert_fusion
  240.1 53.7 %reduce-scatter.3.cloned.1.call-done = f32[16,2048]{1,0:T(8,128)} async-done(((f32[256,2048]{1,0:T(8,128)}), f32[16,2048]{1,0:T(8,128)}) %reduce-scatter.3.cloned.1.call-update) | async-done | bytes 131088 | tf_op jit(solution)/shard_map/reduce_scatter | solution.py:64
  293.8 0.9 fusion.15
  294.7 0.1 copy.18
  294.8 2.4 pad_maximum_fusion
  297.2 1.8 reshape.255
  299.0 10.4 %scatter_custom_fusion.1 = bf16[1024,2048]{1,0:T(8,128)(2,1)} fusion(s32[528]{0:T(1024)S(1)} %fusion.23, bf16[528,2048]{1,0:T(8,128)(2,1)} %reshape.255, bf16[]{:T(256)} %constant.66.clone.1), kind=kCustom, calls=%fused_computation.13 | custom fusion | bytes 4194816 | tf_op jit(solution)/shard_map/scatter | solution.py:73
  309.4 10.7 %all-to-all-start.2 = ((bf16[64,16,2048]{2,1,0:T(8,128)(2,1)}), bf16[64,16,2048]{2,1,0:T(8,128)(2,1)}, u32[]{:S(2)}, u32[]{:S(2)}) async-start(bf16[64,16,2048]{2,1,0:T(8,128)(2,1)} %bitcast.46), calls=%async_computation.3 | async-start | bytes 8388608 | tf_op jit(solution)/shard_map/all_to_all | solution.py:76
  320.1 0.3 reduce-scatter.5.cloned.1.call-start
  320.4 0.5 broadcast.199
  320.9 0.7 reduce.10
  321.6 0.1 reshape.223
  321.7 91.9 %all-to-all-done.2 = bf16[64,16,2048]{2,1,0:T(8,128)(2,1)} async-done(((bf16[64,16,2048]{2,1,0:T(8,128)(2,1)}), bf16[64,16,2048]{2,1,0:T(8,128)(2,1)}, u32[]{:S(2)}, u32[]{:S(2)}) %all-to-all-start.2) | async-done | bytes 4194336 | tf_op jit(solution)/shard_map/all_to_all | solution.py:76
  413.7 18.3 %scatter_custom_fusion.2 = f32[1024,2048]{1,0:T(8,128)} fusion(s32[1024]{0:T(1024)S(1)} %bitcast.56, bf16[1024,2048]{1,0:T(8,128)(2,1)} %bitcast.18, f32[]{:T(128)} %constant.69.clone.1), kind=kCustom, calls=%fused_computation.5 | custom fusion | flops 4194304 | bytes 12582916 | tf_op jit(solution)/shard_map/scatter-add | solution.py:78
  432.0 0.0 copy-start
  432.0 0.0 reduce-scatter.5.cloned.1.call-update
  432.0 0.5 add_subtract_fusion
  432.6 2.4 fusion.6
  434.9 0.0 copy-done
  434.9 0.9 fusion.3
  435.8 78.0 %reduce-scatter.5.cloned.1.call-done = f32[1024,512]{1,0:T(8,128)} async-done(((f32[1024,2048]{1,0:T(8,128)}), f32[1024,512]{1,0:T(8,128)}) %reduce-scatter.5.cloned.1.call-update) | async-done | bytes 2097168 | tf_op jit(solution)/shard_map/reduce_scatter | solution.py:81
  (15 shorter events, 0.2 us)
Async XLA Ops:
  7.2 57.1 %all-gather.4.cloned.1.call-start = ((), (), s32[]{:S(2)}) async-start(), calls=%async_computation.5 | async-start | bytes 5242880 | tf_op jit(solution)/shard_map/all_gather | solution.py:26
  80.3 104.6 %all-to-all-start.1 = ((bf16[64,16,2048]{2,1,0:T(8,128)(2,1)}), bf16[64,16,2048]{2,1,0:T(8,128)(2,1)}, u32[]{:S(2)}, u32[]{:S(2)}) async-start(bf16[64,16,2048]{2,1,0:T(8,128)(2,1)} %broadcast_select_fusion), calls=%async_computation.1 | async-start | bytes 8388608 | tf_op jit(solution)/shard_map/all_to_all | solution.py:29
  91.3 143.0 %all-gather.6.cloned.1.call-start = ((), (), s32[]{:S(2)}) async-start(), calls=%async_computation.8 | async-start | bytes 1114112 | tf_op jit(solution)/shard_map/all_gather | solution.py:34
  193.9 3.9 copy-start.1
  197.6 96.2 %reduce-scatter.3.cloned.1.call-start = ((), (), s32[]{:S(2)}) async-start(), calls=%async_computation.6 | async-start | bytes 2228224 | tf_op jit(solution)/shard_map/reduce_scatter | solution.py:64
  309.4 104.3 %all-to-all-start.2 = ((bf16[64,16,2048]{2,1,0:T(8,128)(2,1)}), bf16[64,16,2048]{2,1,0:T(8,128)(2,1)}, u32[]{:S(2)}, u32[]{:S(2)}) async-start(bf16[64,16,2048]{2,1,0:T(8,128)(2,1)} %bitcast.46), calls=%async_computation.3 | async-start | bytes 8388608 | tf_op jit(solution)/shard_map/all_to_all | solution.py:76
  320.1 193.7 %reduce-scatter.5.cloned.1.call-start = ((), (), s32[]{:S(2)}) async-start(), calls=%async_computation.7 | async-start | bytes 10485760 | tf_op jit(solution)/shard_map/reduce_scatter | solution.py:81
  432.0 2.9 copy-start
Sparse Core Ops, SparseCore 0:
  9.8 54.3 all-gather.3
  197.7 36.6 all-gather.5
  238.3 55.4 reduce-scatter.2
  432.2 81.6 reduce-scatter.4
where the time goes:
time: 521 us; the launch traced here: 520 us
  waiting for transfers between devices  378 us (73%)
  local copies, waits for them, and re-layouts  42.5 us (8%)
  other arithmetic  32.2 us (6%)
  starting transfers between devices  22.3 us (4%)
  blocking collectives  22 us (4%)
  between operations  14 us (3%)
  matrix products  9.2 us (2%)
    all_to_all x1, waiting for transfers between devices, body(): lax.all_to_all(found, ('dp', 'corpus'), split_axis=0, concat_axis=0, tile...  93.5 us
    all_to_all x1, waiting for transfers between devices, body(): lax.all_to_all(grad_slots, ('dp', 'corpus'), split_axis=0, concat_axis=0,...  91.9 us
    reduce_scatter x1, waiting for transfers between devices, body(): lax.psum_scatter(accum_grad, 'tensor', scatter_dimension=1, tiled=True)  78 us
    reduce_scatter x1, waiting for transfers between devices, body(): lax.psum_scatter(in_terms, 'dp', scatter_dimension=0, tiled=True)  53.7 us
    all_gather x1, waiting for transfers between devices, body(): in_batch = lax.all_gather(pos_rows, 'dp', axis=0, tiled=True)  34 us
    all_gather x1, waiting for transfers between devices, body(): row_table = lax.all_gather(passages, 'tensor', axis=1, tiled=True)  26.3 us
    all_to_all x1, blocking collectives, body(): lax.all_to_all(send_ids, ('dp', 'corpus'), split_axis=0, concat_axis=0, t...  22 us
    scatter-add x1, other arithmetic, body(): accum_grad.at[asked_ids.reshape(-1)]  18.3 us
  transfers between devices with their start and end apart: 6, of which 6 were waited for; matrix products, arithmetic and copies ran while one was open for 3% of the time, Pallas kernels for 0%

commit v1 on v0

v1 whole, which is shorter than its diff:
```python
import jax
import jax.numpy as jnp
from jax import lax
from jax.sharding import PartitionSpec as P

CAP = 16


def gather_queries(queries):
    n_dp, n_t, n_c = (lax.axis_size(a) for a in ("dp", "tensor", "corpus"))
    qd, feat = queries.shape
    width = feat // n_t
    mine = queries.reshape(qd, n_t, width).swapaxes(0, 1)
    mine = lax.all_to_all(mine, "tensor", split_axis=0, concat_axis=0, tiled=True)
    every = lax.all_gather(mine, ("dp", "corpus"), axis=0, tiled=False)
    every = every.reshape(n_dp, n_c, n_t, qd, width).transpose(2, 1, 0, 3, 4)
    return every.reshape(n_t * n_c, n_dp * qd, width)


def gather_small(values):
    n_dp, n_t, n_c = (lax.axis_size(a) for a in ("dp", "tensor", "corpus"))
    every = lax.all_gather(values, ("dp", "tensor", "corpus"), axis=0, tiled=False)
    every = every.reshape((n_dp, n_t * n_c) + values.shape)
    return jnp.swapaxes(every, 0, 1)


def scatter_scores(part):
    n_groups, n_dp = part.shape[:2]
    part = jnp.swapaxes(part, 0, 1).reshape((n_dp * n_groups,) + part.shape[2:])
    return lax.psum_scatter(part, ("dp", "tensor", "corpus"), scatter_dimension=0, tiled=False)


def scatter_grads(part):
    n_dp, n_t, n_c = (lax.axis_size(a) for a in ("dp", "tensor", "corpus"))
    n_groups, members, width = part.shape
    qd = members // n_dp
    part = part.reshape(n_t, n_c, n_dp, qd, width).transpose(2, 1, 0, 3, 4)
    part = part.reshape(n_dp * n_c, n_t, qd, width)
    mine = lax.psum_scatter(part, ("dp", "corpus"), scatter_dimension=0, tiled=False)
    mine = lax.all_to_all(mine, "tensor", split_axis=0, concat_axis=0, tiled=True)
    return mine.swapaxes(0, 1).reshape(qd, n_t * width)


def body(queries, passages, pos_ids, neg_ids):
    n_dp, n_t, n_c = (lax.axis_size(a) for a in ("dp", "tensor", "corpus"))
    qd, feat = queries.shape
    block_rows, width = passages.shape
    neg_count = neg_ids.shape[1]
    n_groups = n_t * n_c
    members = n_dp * qd
    items = (neg_count + 1) * qd
    scale = feat ** (-0.5)
    f32, bf16 = jnp.float32, jnp.bfloat16
    block = lax.axis_index("dp") * n_c + lax.axis_index("corpus")

    ids = jnp.concatenate([pos_ids[None, :], neg_ids.T], axis=0).reshape(items)
    every_id = gather_small(ids)
    every_query = gather_queries(queries)

    item_no = jnp.arange(items, dtype=jnp.int32)
    match = every_id // block_rows == block
    before = (item_no[:, None] < item_no[None, :]).astype(bf16)
    rank = jnp.einsum("gdj,jk->gdk", match.astype(bf16), before, preferred_element_type=f32)
    rank = jnp.where(match, rank.astype(jnp.int32), -1)
    packed = (every_id % block_rows) * items + item_no + 1
    slot_no = jnp.arange(CAP, dtype=jnp.int32)
    held = jnp.sum(
        jnp.where(rank[:, :, None, :] == slot_no[:, None], packed[:, :, None, :], 0), axis=3
    )
    full = held > 0
    row = jnp.where(full, (held - 1) // items, -1)
    item = jnp.where(full, (held - 1) % items, -1)
    slots = n_dp * CAP
    own = jnp.arange(n_dp, dtype=jnp.int32)[:, None] * qd + item % qd
    own = jnp.where(full, own, -1).reshape(n_groups, slots)
    is_pos = (full & (item < qd)).reshape(n_groups, slots)
    member_no = jnp.arange(members, dtype=jnp.int32)
    onehot = (row.reshape(n_groups, slots)[:, :, None] == jnp.arange(block_rows)).astype(bf16)
    at_own = own[:, :, None] == member_no
    pick_pos = (at_own & is_pos[:, :, None]).astype(bf16)
    at_neg = at_own & ~is_pos[:, :, None]

    rows = jnp.einsum("gsp,pw->gsw", onehot, passages, preferred_element_type=f32).astype(bf16)
    pos_rows = jnp.einsum("gsc,gsw->gcw", pick_pos, rows, preferred_element_type=f32).astype(bf16)
    in_part = jnp.einsum("gqw,gcw->gqc", every_query, pos_rows, preferred_element_type=f32)
    slot_part = jnp.einsum("gsw,gqw->gsq", rows, every_query, preferred_element_type=f32)
    score = jnp.sum(jnp.where(at_neg, slot_part, 0.0), axis=2).reshape(n_groups, n_dp, CAP)
    neg_no = item_no[qd:]
    neg_part = jnp.sum(
        jnp.where(item[:, :, :, None] == neg_no, score[:, :, :, None], 0.0), axis=2
    )
    neg_part = neg_part.reshape(n_groups, n_dp, neg_count, qd).swapaxes(2, 3)
    part = jnp.concatenate([in_part.reshape(n_groups, n_dp, qd, members), neg_part], axis=3)
    logits = scatter_scores(part) * scale

    row_max = jnp.max(logits, axis=1, keepdims=True)
    exponent = jnp.exp(logits - row_max)
    denominator = jnp.sum(exponent, axis=1, keepdims=True)
    own_col = lax.axis_index("dp") * qd + jnp.arange(qd)
    target = (jnp.arange(members + neg_count)[None, :] == own_col[:, None]).astype(f32)
    losses = jnp.log(denominator[:, 0]) + row_max[:, 0] - jnp.sum(target * logits, axis=1)
    weights = (exponent / denominator - target).astype(bf16)

    every_weight = gather_small(weights)
    in_weights = every_weight[..., :members].reshape(n_groups, members, members)
    neg_weights = every_weight[..., members:].swapaxes(2, 3).reshape(n_groups, n_dp, -1)
    slot_weight = jnp.sum(
        jnp.where(
            item[:, :, :, None] == neg_no, neg_weights[:, :, None, :].astype(f32), 0.0
        ),
        axis=3,
    ).reshape(n_groups, slots)
    spread = jnp.einsum("gsc,gqc->gsq", pick_pos, in_weights, preferred_element_type=f32)
    spread = jnp.where(at_neg, slot_weight[:, :, None], spread).astype(bf16)
    slot_grads = jnp.einsum("gsq,gqw->gsw", spread, every_query, preferred_element_type=f32)
    slot_grads = (slot_grads * scale).astype(bf16)
    grad_pass = jnp.einsum("gsp,gsw->pw", onehot, slot_grads, preferred_element_type=f32)
    query_part = jnp.einsum("gsq,gsw->gqw", spread, rows, preferred_element_type=f32)
    grad_query = scatter_grads(query_part * scale)
    return (grad_query, losses, grad_pass)


def solution(mesh):
    in_specs = (
        P(("dp", "tensor", "corpus"), None),
        P(("dp", "corpus"), "tensor"),
        P(("dp", "tensor", "corpus")),
        P(("dp", "tensor", "corpus"), None),
    )
    out_specs = (
        P(("dp", "tensor", "corpus"), None),
        P(("dp", "tensor", "corpus")),
        P(("dp", "corpus"), "tensor"),
    )
    return jax.shard_map(body, mesh=mesh, in_specs=in_specs, out_specs=out_specs, check_vma=False)
```

time: 521 us -> 892 us (1.71)
  waiting for transfers between devices: 378 us -> 649 us
  blocking collectives: 22 us -> 140 us
  matrix products: 9.2 us -> 30.9 us
  starting transfers between devices: 22.3 us -> 4.61 us
  local copies, waits for them, and re-layouts: 42.5 us -> 28.8 us
  other arithmetic: 32.2 us -> 20.3 us
    reduce_scatter x2, waiting for transfers between devices: 132 us -> 539 us  [the longest x1 394 us: scatter_scores(): lax.psum_scatter(part, ('dp', 'tensor', 'corpus'), scatter_dimension=0, t...]
    all_to_all x2 -> x1, waiting for transfers between devices: 185 us -> 0.01 us  [scatter_grads(): lax.all_to_all(mine, 'tensor', split_axis=0, concat_axis=0, tiled=True)]
    all_gather x0 -> x1, blocking collectives: none -> 130 us  [gather_small(): lax.all_gather(values, ('dp', 'tensor', 'corpus'), axis=0, tiled=False)]
    all_gather x2, waiting for transfers between devices: 60.3 us -> 109 us  [the longest x1 109 us: gather_small(): lax.all_gather(values, ('dp', 'tensor', 'corpus'), axis=0, tiled=False)]
    dot_general x5 -> x7, matrix products: 9.2 us -> 30.9 us  [the longest x1 9.24 us: body(): jnp.einsum('gsp,gsw->pw', onehot, slot_grads, preferred_element_type=f32)]
    gather x2 -> x0, local copies, waits for them, and re-layouts: 20.6 us -> none  [the longest x1 11.6 us: lookup_rows(): return jnp.take(row_table, asked_ids, axis=0, mode='fill', fill_value=0)]
    scatter-add x1 -> x0, other arithmetic: 18.3 us -> none  [body(): accum_grad.at[asked_ids.reshape(-1)]]
    all_to_all x2 -> x1, starting transfers between devices: 21.8 us -> 4.44 us  [scatter_grads(): lax.all_to_all(mine, 'tensor', split_axis=0, concat_axis=0, tiled=True)]
  transfers between devices with their start and end apart: 6 -> 5, of which waited for: 6 -> 3; matrix products, arithmetic and copies ran while one was open for 3% -> 3% of each run, Pallas kernels for 0% -> 0%
where the time goes in v1:
time: 892 us; the launch traced here: 887 us
  waiting for transfers between devices  649 us (73%)
  blocking collectives  140 us (16%)
  matrix products  30.9 us (3%)
  local copies, waits for them, and re-layouts  28.8 us (3%)
  other arithmetic  20.3 us (2%)
  between operations  14 us (2%)
    reduce_scatter x1, waiting for transfers between devices, scatter_scores(): lax.psum_scatter(part, ('dp', 'tensor', 'corpus'), scatter_dimension=0, t...  394 us
    reduce_scatter x1, waiting for transfers between devices, scatter_grads(): lax.psum_scatter(part, ('dp', 'corpus'), scatter_dimension=0, tiled=False)  146 us
    all_gather x1, blocking collectives, gather_small(): lax.all_gather(values, ('dp', 'tensor', 'corpus'), axis=0, tiled=False)  130 us
    all_gather x1, waiting for transfers between devices, gather_small(): lax.all_gather(values, ('dp', 'tensor', 'corpus'), axis=0, tiled=False)  109 us
  transfers between devices with their start and end apart: 5, of which 3 were waited for; matrix products, arithmetic and copies ran while one was open for 3% of the time, Pallas kernels for 0%

profile of v1, /device:TPU:1, one launch (start us, length us, event | category | flops | bytes accessed | tf_op | source)
XLA Modules:
  0.0 887.3 jit_solution(11507428779567494971)
XLA Ops:
  7.2 0.0 copy-start
  7.2 0.0 all-gather.7.cloned.1.call-start
  7.2 1.0 reshape.199
  8.2 9.4 %all_to_all.10 = bf16[4,16,512]{2,1,0:T(8,128)(2,1)} all-to-all(bf16[4,16,512]{2,1,0:T(8,128)(2,1)S(1)} %copy.57), channel_id=1, replica_groups=mesh['dp'=16,'tensor'=4,'corpus'=4] {'tensor'}, dimensions={0} | all-to-all | bytes 131072 | tf_op jit(solution)/shard_map/all_to_all | solution.py:14
  17.6 0.0 all-gather.7.cloned.1.call-update
  17.6 0.0 reduce-scatter.3.cloned.1.call-start
  17.7 0.1 slice.9
  17.8 0.1 add.116
  17.8 0.1 add.117
  17.9 0.7 copy.53
  18.6 0.8 pad_add_fusion
  19.4 0.1 copy.54
  19.5 0.1 reshape.213
  19.6 130.4 %all-gather.1 = s32[256,1,528]{2,1,0:T(1,128)S(1)} all-gather(s32[1,1,528]{2,1,0:T(1,128)S(1)} %reshape.213), channel_id=1, replica_groups=mesh['dp'=16,'tensor'=4,'corpus'=4] {'dp','tensor','corpus'}, dimensions={0}, use_global_device_ids=true | all-gather | bytes 542784 | tf_op jit(solution)/shard_map/all_gather | solution.py:22
  150.1 0.4 fusion.44
  150.5 1.1 fusion.37
  151.6 4.4 select_reduce_fusion
  156.1 0.1 ne.103
  156.2 0.1 add_remainder_fusion
  156.3 0.1 rem.88
  156.4 0.1 gt.31
  156.5 0.1 div.39
  156.7 0.0 copy-done
  156.7 6.3 fusion.21
  163.0 0.0 all-gather.7.cloned.1.call-done
  163.0 2.8 copy.58
  165.8 0.0 copy-start.4
  165.8 1.9 copy-done.4
  167.8 0.0 copy-done.2
  167.8 1.5 select_reduce_fusion.1
  169.3 0.1 broadcast_in_dim.80
  169.4 2.5 fusion.2
  171.9 2.8 reshape.203
  174.7 2.8 copy.60
  177.5 7.8 fusion.7
  185.3 5.5 pad_maximum_fusion
  190.8 0.0 reduce-scatter.3.cloned.1.call-update
  190.9 0.0 all-gather.5.cloned.1.call-start
  190.9 393.6 %reduce-scatter.3.cloned.1.call-done = f32[1,16,288]{2,1,0:T(8,128)} async-done(((f32[256,16,288]{2,1,0:T(8,128)}), f32[1,16,288]{2,1,0:T(8,128)}) %reduce-scatter.3.cloned.1.call-update) | async-done | bytes 18448 | tf_op jit(solution)/shard_map/reduce_scatter | solution.py:30
  584.5 0.9 multiply_reduce_fusion
  585.4 0.9 fusion.60
  586.3 1.4 subtract_convert_fusion
  587.7 0.0 all-gather.5.cloned.1.call-update
  587.7 0.0 reduce-scatter.5.cloned.1.call-start
  587.8 109.4 %all-gather.5.cloned.1.call-done = bf16[256,16,288]{2,1,0:T(8,128)(2,1)} async-done(((bf16[1,16,288]{2,1,0:T(8,128)(2,1)}), bf16[256,16,288]{2,1,0:T(8,128)(2,1)}) %all-gather.5.cloned.1.call-update) | async-done | bytes 2359312 | tf_op jit(solution)/shard_map/all_gather | solution.py:22
  697.2 1.8 slice.13
  699.0 1.5 convert_bitcast_fusion
  700.5 1.5 copy.62
  702.0 2.8 copy.61
  704.8 4.5 reshape.210
  709.3 1.4 fusion.3
  710.7 0.1 broadcast_in_dim.84
  710.8 3.7 select_convert_fusion
  714.5 0.0 copy-done.3
  714.5 1.3 broadcast_multiply_fusion
  715.8 4.3 copy.65
  720.1 0.0 reduce-scatter.5.cloned.1.call-update
  720.1 0.5 add_subtract_fusion
  720.7 145.8 %reduce-scatter.5.cloned.1.call-done = f32[1,4,16,512]{3,2,1,0:T(8,128)} async-done(((f32[64,4,16,512]{3,2,1,0:T(8,128)}), f32[1,4,16,512]{3,2,1,0:T(8,128)}) %reduce-scatter.5.cloned.1.call-update) | async-done | bytes 131088 | tf_op jit(solution)/shard_map/reduce_scatter | solution.py:39
  866.5 4.4 all-to-all-start.1
  870.9 9.2 %fusion.30 = f32[1024,512]{1,0:T(8,128)} fusion(bf16[16,256,256]{1,2,0:T(8,128)(2,1)S(1)} %select_convert_fusion, bf16[16,256,512]{2,1,0:T(8,128)(2,1)} %bitcast.110, s32[16,256]{1,0:T(8,128)S(1)} %get-tuple-element.14), kind=kOutput, calls=%fused_computation.31 | convolution fusion | flops 5377097728 | bytes 8404992 | tf_op jit(solution)/shard_map/gsp,gsw->pw/dot_general | solution.py:117
  880.1 0.0 all-to-all-done.1
  880.1 0.7 copy.73
  880.8 0.0 copy-done.1
  (11 shorter events, 0.2 us)
Async XLA Ops:
  7.2 149.5 %copy-start = (bf16[1024,512]{1,0:T(8,128)(2,1)S(1)}, bf16[1024,512]{1,0:T(8,128)(2,1)}, u32[]{:S(2)}) copy-start(bf16[1024,512]{1,0:T(8,128)(2,1)} %param.5) | copy-start | bytes 3145732
  7.2 155.8 %all-gather.7.cloned.1.call-start = ((), (), s32[]{:S(2)}) async-start(), calls=%async_computation.7 | async-start | bytes 4259840 | tf_op jit(solution)/shard_map/all_gather | solution.py:15
  17.6 566.9 %reduce-scatter.3.cloned.1.call-start = ((), (), s32[]{:S(2)}) async-start(), calls=%async_computation.4 | async-start | bytes 6316032 | tf_op jit(solution)/shard_map/reduce_scatter | solution.py:30
  163.0 4.7 copy-start.2
  165.8 1.9 copy-start.4
  190.9 506.4 %all-gather.5.cloned.1.call-start = ((), (), s32[]{:S(2)}) async-start(), calls=%async_computation.5 | async-start | bytes 3158016 | tf_op jit(solution)/shard_map/all_gather | solution.py:22
  587.7 278.7 %reduce-scatter.5.cloned.1.call-start = ((), (), s32[]{:S(2)}) async-start(), calls=%async_computation.6 | async-start | bytes 8519680 | tf_op jit(solution)/shard_map/reduce_scatter | solution.py:39
  710.8 3.7 copy-start.3
  866.5 13.7 %all-to-all-start.1 = ((f32[4,16,512]{2,1,0:T(8,128)}), f32[4,16,512]{2,1,0:T(8,128)S(1)}, u32[]{:S(2)}, u32[]{:S(2)}) async-start(f32[4,16,512]{2,1,0:T(8,128)} %bitcast.119), calls=%async_computation.3 | async-start | bytes 262144 | tf_op jit(solution)/shard_map/all_to_all | solution.py:40
  870.9 9.9 %copy-start.1 = (bf16[1024,512]{1,0:T(8,128)(2,1)S(1)}, bf16[1024,512]{1,0:T(8,128)(2,1)}, u32[]{:S(2)}) copy-start(bf16[1024,512]{1,0:T(8,128)(2,1)} %param.5) | copy-start | bytes 3145732
Sparse Core Ops, SparseCore 0:
  17.7 81.9 all-gather.6
  191.0 393.4 reduce-scatter.2
  588.6 108.5 all-gather.4
  720.3 146.1 reduce-scatter.4

commit v2 on v1

v2 whole, which is shorter than its diff:
```python
import functools

import jax
import jax.numpy as jnp
from jax import lax
from jax.experimental import pallas as pl
from jax.experimental.pallas import tpu as pltpu
from jax.sharding import PartitionSpec as P

CAP = 16
VMEM_LIMIT = 62 * 1024 * 1024
CORES = 2


class Place:
    def __init__(self):
        dp = lax.axis_index("dp")
        self.size = {
            "z": lax.axis_size("dp") // CORES,
            "tensor": lax.axis_size("tensor"),
            "corpus": lax.axis_size("corpus"),
        }
        self.at = {
            "z": dp // CORES,
            "tensor": lax.axis_index("tensor"),
            "corpus": lax.axis_index("corpus"),
        }
        self.core = dp % CORES

    def along(self, axis, step):
        n = self.size[axis]
        return lax.rem(self.at[axis] + (step + n), n)

    def device(self, axis, step):
        if axis == "core":
            return {"dp": self.at["z"] * CORES + (1 - self.core)}
        spot = self.along(axis, step)
        if axis == "z":
            return {"dp": spot * CORES + self.core}
        return {axis: spot}

    def greet(self, peers):
        barrier = pltpu.get_barrier_semaphore()
        for axis, step in peers:
            pl.semaphore_signal(
                barrier, inc=1, device_id=self.device(axis, step),
                device_id_type=pl.DeviceIdType.MESH,
            )
        pl.semaphore_wait(barrier, len(peers))


class Wire:
    def __init__(self, send_sem, recv_sem):
        self.send_sem, self.recv_sem = send_sem, recv_sem
        self.used = 0
        self.sent = []

    def make(self, src, dst, device, number):
        return pltpu.make_async_remote_copy(
            src_ref=src, dst_ref=dst, send_sem=self.send_sem.at[number],
            recv_sem=self.recv_sem.at[number], device_id=device,
            device_id_type=pl.DeviceIdType.MESH,
        )

    def send(self, src, dst, device, landing):
        number = self.used
        self.used += 1
        copy = self.make(src, dst, device, number)
        copy.start()
        self.sent.append(copy)
        return self.make(landing, landing, device, number)

    def finish(self):
        for copy in self.sent:
            copy.wait_send()


def interleave(walks):
    walks = list(walks)
    while walks:
        for walk in list(walks):
            try:
                next(walk)
            except StopIteration:
                walks.remove(walk)


def add_to(dst, first, others):
    lead = 1
    for n in dst.shape[:-2]:
        lead *= n
    if len(dst.shape) > 2 and lead * dst.shape[-2] * dst.shape[-1] > 32 * 1024:
        def step(i, carry):
            add_to(dst.at[i], first.at[i], [o.at[i] for o in others])
            return carry
        lax.fori_loop(0, dst.shape[0], step, 0)
        return
    total = first[...]
    for o in others:
        total = total + o[...]
    dst[...] = total


def ring_gather(place, wire, view, axes, flip, swap):
    for stage, axis in enumerate(axes):
        n = place.size[axis]
        last = stage == len(axes) - 1
        def at(step, axis=axis, stage=stage):
            where = {}
            for a in axes[:stage]:
                where[a] = slice(None)
            where[axis] = place.along(axis, step)
            for a in axes[stage + 1:]:
                where[a] = place.at[a]
            return where
        far = n // 2
        near = n - 1 - far
        hops = {1: near, -1: far} if flip else {1: far, -1: near}
        if last:
            swap(at(0))
        landed = {1: None, -1: None}
        for s in range(far):
            for way in (1, -1):
                if s < hops[way]:
                    if landed[way] is not None:
                        landed[way].wait_recv()
                        if last:
                            swap(at(-way * s))
                    block = view(at(-way * s), place.core)
                    coming = view(at(-way * (s + 1)), place.core)
                    landed[way] = wire.send(block, block, place.device(axis, way), coming)
            yield
        for way in (1, -1):
            if landed[way] is not None:
                landed[way].wait_recv()
                if last:
                    swap(at(-way * hops[way]))
        yield


def ring_reduce(place, wire, held, dims, axes, boxes, holds, flip, out):
    dims = list(dims)
    for stage, axis in enumerate(axes):
        n = place.size[axis]
        spot = dims.index(axis)

        def at(step, held=held, spot=spot, axis=axis):
            return held.at[(slice(None),) * spot + (place.along(axis, step),)]

        box = boxes[stage]
        far = n // 2
        near = n - 1 - far
        hops = {1: near, -1: far} if flip else {1: far, -1: near}
        base = {1: 0, -1: hops[1]}
        landed = {}
        for s in range(far):
            for way in (1, -1):
                if s < hops[way]:
                    source = at(way * (hops[way] - s))
                    if s > 0:
                        landed[way].wait_recv()
                        got = box.at[base[way] + s - 1]
                        add_to(got, got, [source])
                        source = got
                    slot = box.at[base[way] + s]
                    landed[way] = wire.send(source, slot, place.device(axis, way), slot)
            yield
        terms = []
        for way in (1, -1):
            if hops[way]:
                landed[way].wait_recv()
                terms.append(box.at[base[way] + hops[way] - 1])
        target = out if stage == len(axes) - 1 else holds[stage]
        add_to(target, at(0), terms)
        held = target
        dims.pop(spot)
        yield


def fold_cores(place, wire, part, box, lead):
    every = (slice(None),) * lead
    landing = wire.send(part.at[every + (1 - place.core,)], box, place.device("core", 1), box)
    yield
    landing.wait_recv()
    add_to(box, box, [part.at[every + (place.core,)]])
    yield


def reduce_walk(place, wire, part, box, dims, axes, boxes, holds, flip, out):
    yield from fold_cores(place, wire, part, box, len(dims))
    yield from ring_reduce(place, wire, box, dims, axes, boxes, holds, flip, out)


def reduce_scratch(sizes, dims, axes, chunk):
    def buffer(lead):
        return pltpu.VMEM(tuple(lead) + tuple(chunk), jnp.float32)

    left = list(dims)
    fold = buffer([sizes[d] for d in left])
    boxes, holds = [], []
    for stage, axis in enumerate(axes):
        left.remove(axis)
        part = [sizes[d] for d in left]
        boxes.append(buffer([sizes[axis] - 1] + part))
        if stage < len(axes) - 1:
            holds.append(buffer(part))
    return [fold] + boxes + holds


def split_scratch(refs, stages):
    return refs[0], refs[1:1 + stages], refs[1 + stages:2 * stages]


def mesh_sizes():
    return {
        "z": lax.axis_size("dp") // CORES,
        "tensor": lax.axis_size("tensor"),
        "corpus": lax.axis_size("corpus"),
    }


def ring_peers(axes):
    return [("core", 1)] + [(a, way) for a in axes for way in (1, -1)]


VMEM_SPEC = pl.BlockSpec(memory_space=pltpu.VMEM)


def kernel_call(kernel, outs, scratch, copies, number, inputs):
    return pl.pallas_call(
        kernel,
        out_shape=outs,
        in_specs=[VMEM_SPEC] * len(inputs),
        out_specs=[VMEM_SPEC] * len(outs),
        scratch_shapes=[
            pltpu.SemaphoreType.DMA((copies,)),
            pltpu.SemaphoreType.DMA((copies,)),
        ] + scratch,
        compiler_params=pltpu.CompilerParams(
            collective_id=number, has_side_effects=True, vmem_limit_bytes=VMEM_LIMIT
        ),
    )(*inputs)


def swapper(place, wire, view, waits):
    def swap(where):
        block = view(where, place.core)
        landing = view(where, 1 - place.core)
        waits.append(wire.send(block, block, place.device("core", 1), landing))
    return swap


def query_kernel(q_in, ids_in, q_out, ids_out, send_sem, recv_sem, own_sem):
    place = Place()
    wire = Wire(send_sem, recv_sem)
    n_t = place.size["tensor"]
    t, c, z, core = place.at["tensor"], place.at["corpus"], place.at["z"], place.core
    place.greet(ring_peers(("z", "corpus")) + [("tensor", o) for o in range(1, n_t)])
    keep = [
        pltpu.make_async_copy(q_in.at[t], q_out.at[t, c, z, core], own_sem.at[0]),
        pltpu.make_async_copy(ids_in, ids_out.at[t, c, z, core], own_sem.at[1]),
    ]
    for copy in keep:
        copy.start()
    landings = []
    for o in range(1, n_t):
        peer, source = place.along("tensor", o), place.along("tensor", -o)
        device = place.device("tensor", o)
        landings.append(wire.send(
            q_in.at[peer], q_out.at[t, c, z, core], device, q_out.at[source, c, z, core]
        ))
        landings.append(wire.send(
            ids_in, ids_out.at[t, c, z, core], device, ids_out.at[source, c, z, core]
        ))
    for copy in keep:
        copy.wait()
    for landing in landings:
        landing.wait_recv()
    half = n_t // 2

    def of(ref, part):
        return lambda where, k: ref.at[part, where["corpus"], where["z"], k]

    waits, walks = [], []
    for ref, part, axes, flip in (
        (ids_out, slice(0, n_t), ("corpus", "z"), True),
        (q_out, slice(0, half), ("corpus", "z"), False),
        (q_out, slice(half, n_t), ("z", "corpus"), True),
    ):
        view = of(ref, part)
        walks.append(ring_gather(
            place, wire, view, axes, flip, swapper(place, wire, view, waits)
        ))
    interleave(walks)
    for landing in waits:
        landing.wait_recv()
    wire.finish()


def gather_queries(queries, ids):
    sizes = mesh_sizes()
    n_t, n_c, n_z = sizes["tensor"], sizes["corpus"], sizes["z"]
    qd, feat = queries.shape
    width = feat // n_t
    mine = queries.reshape(qd, n_t, width).swapaxes(0, 1)
    lead = (n_t, n_c, n_z, CORES)
    count = ids.shape[1]
    copies = 2 * (n_t - 1) + 3 * (n_c + n_z - 2) + 2 * n_z + n_c
    every_query, every_id = kernel_call(
        query_kernel,
        [
            jax.ShapeDtypeStruct(lead + (qd, width), queries.dtype),
            jax.ShapeDtypeStruct(lead + (1, count), ids.dtype),
        ],
        [pltpu.SemaphoreType.DMA((2,))], copies, 0, (mine, ids),
    )
    groups, members = n_t * n_c, n_z * CORES
    return (
        every_query.reshape(groups, members * qd, width),
        every_id.reshape(groups, members, count),
    )


WEIGHT_WALKS = (
    (("tensor", "corpus", "z"), False),
    (("z", "tensor", "corpus"), True),
    (("corpus", "z", "tensor"), False),
)


def weight_kernel(*refs):
    parts = len(WEIGHT_WALKS)
    ins, outs = refs[:parts], refs[parts:2 * parts]
    send_sem, recv_sem, own_sem = refs[2 * parts:]
    place = Place()
    wire = Wire(send_sem, recv_sem)
    t, c, z, core = place.at["tensor"], place.at["corpus"], place.at["z"], place.core
    place.greet(ring_peers(("z", "corpus", "tensor")))
    keep = [
        pltpu.make_async_copy(i, o.at[t, c, z, core], own_sem.at[n])
        for n, (i, o) in enumerate(zip(ins, outs))
    ]
    for copy in keep:
        copy.start()
    for copy in keep:
        copy.wait()

    def of(ref):
        return lambda where, k: ref.at[where["tensor"], where["corpus"], where["z"], k]

    waits, walks = [], []
    for out, (axes, flip) in zip(outs, WEIGHT_WALKS):
        view = of(out)
        walks.append(ring_gather(
            place, wire, view, axes, flip, swapper(place, wire, view, waits)
        ))
    interleave(walks)
    for landing in waits:
        landing.wait_recv()
    wire.finish()


def gather_weights(parts):
    sizes = mesh_sizes()
    lead = (sizes["tensor"], sizes["corpus"], sizes["z"], CORES)
    hops = sum(sizes.values()) - 3
    copies = sum(hops + sizes[axes[-1]] for axes, _ in WEIGHT_WALKS)
    return kernel_call(
        weight_kernel,
        [jax.ShapeDtypeStruct(lead + p.shape, p.dtype) for p in parts],
        [pltpu.SemaphoreType.DMA((len(parts),))], copies, 1, tuple(parts),
    )


SCORE_DIMS = ("tensor", "corpus", "z")
SCORE_WALKS = (
    (("tensor", "z", "corpus"), False),
    (("z", "corpus", "tensor"), True),
    (("corpus", "tensor", "z"), False),
)


def score_kernel(*refs):
    parts = len(SCORE_WALKS)
    ins, outs = refs[:parts], refs[parts:2 * parts]
    send_sem, recv_sem = refs[2 * parts:2 * parts + 2]
    scratch = refs[2 * parts + 2:]
    place = Place()
    wire = Wire(send_sem, recv_sem)
    place.greet(ring_peers(SCORE_DIMS))
    each = len(scratch) // parts
    walks = []
    for n, (axes, flip) in enumerate(SCORE_WALKS):
        fold, boxes, holds = split_scratch(scratch[n * each:(n + 1) * each], len(axes))
        walks.append(reduce_walk(
            place, wire, ins[n], fold, SCORE_DIMS, axes, boxes, holds, flip, outs[n]
        ))
    interleave(walks)
    wire.finish()


def scatter_scores(parts):
    sizes = mesh_sizes()
    scratch = []
    chunks = [p.shape[4:] for p in parts]
    for chunk, (axes, _) in zip(chunks, SCORE_WALKS):
        scratch += reduce_scratch(sizes, SCORE_DIMS, axes, chunk)
    copies = len(parts) * (sum(sizes.values()) - 2)
    return kernel_call(
        score_kernel, [jax.ShapeDtypeStruct(c, jnp.float32) for c in chunks],
        scratch, copies, 2, tuple(parts),
    )


GRAD_DIMS = ("corpus", "z")
GRAD_WALKS = ((("corpus", "z"), False), (("z", "corpus"), True))


def grad_kernel(*refs):
    parts = len(GRAD_WALKS)
    ins, out = refs[:parts], refs[parts]
    send_sem, recv_sem, own_sem, done = refs[parts + 1:parts + 5]
    scratch = refs[parts + 5:]
    place = Place()
    wire = Wire(send_sem, recv_sem)
    n_t, t = place.size["tensor"], place.at["tensor"]
    place.greet(ring_peers(GRAD_DIMS) + [("tensor", o) for o in range(1, n_t)])
    each = len(scratch) // parts
    share = n_t // parts
    walks = []
    for n, (axes, flip) in enumerate(GRAD_WALKS):
        fold, boxes, holds = split_scratch(scratch[n * each:(n + 1) * each], len(axes))
        walks.append(reduce_walk(
            place, wire, ins[n], fold, GRAD_DIMS, axes, boxes, holds, flip,
            done.at[n * share:(n + 1) * share],
        ))
    interleave(walks)
    keep = pltpu.make_async_copy(done.at[t], out.at[t], own_sem.at[0])
    keep.start()
    landings = []
    for o in range(1, n_t):
        peer, source = place.along("tensor", o), place.along("tensor", -o)
        landings.append(wire.send(
            done.at[peer], out.at[t], place.device("tensor", o), out.at[source]
        ))
    keep.wait()
    for landing in landings:
        landing.wait_recv()
    wire.finish()


def scatter_grads(parts):
    sizes = mesh_sizes()
    share, qd, width = parts[0].shape[3:]
    n_t = sizes["tensor"]
    scratch = [pltpu.SemaphoreType.DMA((1,)), pltpu.VMEM((n_t, qd, width), jnp.float32)]
    for axes, _ in GRAD_WALKS:
        scratch += reduce_scratch(sizes, GRAD_DIMS, axes, (share, qd, width))
    copies = len(parts) * (sizes["corpus"] + sizes["z"] - 1) + n_t - 1
    (mine,) = kernel_call(
        grad_kernel, [jax.ShapeDtypeStruct((n_t, qd, width), jnp.float32)],
        scratch, copies, 3, tuple(parts),
    )
    return mine.swapaxes(0, 1).reshape(qd, n_t * width)


def body(queries, passages, pos_ids, neg_ids):
    sizes = mesh_sizes()
    n_t, n_c, n_z = sizes["tensor"], sizes["corpus"], sizes["z"]
    n_dp = n_z * CORES
    qd, feat = queries.shape
    block_rows, width = passages.shape
    neg_count = neg_ids.shape[1]
    n_groups = n_t * n_c
    members = n_dp * qd
    items = (neg_count + 1) * qd
    padded = -(-(items + 1) // 128) * 128
    scale = feat ** (-0.5)
    f32, bf16 = jnp.float32, jnp.bfloat16
    block = lax.axis_index("dp") * n_c + lax.axis_index("corpus")
    lead = (n_t, n_c, n_z, CORES)

    ids = jnp.concatenate([pos_ids[None, :], neg_ids.T], axis=0).reshape(1, items)
    ids = jnp.pad(ids, ((0, 0), (0, padded - items)), constant_values=-1)
    every_query, every_id = gather_queries(queries, ids)

    item_no = jnp.arange(padded, dtype=jnp.int32)
    match = every_id // block_rows == block
    before = (item_no[:, None] < item_no[None, :]).astype(bf16)
    rank = jnp.einsum("gdj,jk->gdk", match.astype(bf16), before, preferred_element_type=f32)
    rank = jnp.where(match, rank.astype(jnp.int32), -1)
    packed = (every_id % block_rows) * padded + item_no + 1
    slot_no = jnp.arange(CAP, dtype=jnp.int32)
    held = jnp.sum(
        jnp.where(rank[:, :, None, :] == slot_no[:, None], packed[:, :, None, :], 0), axis=3
    )
    full = held > 0
    row = jnp.where(full, (held - 1) // padded, -1)
    item = jnp.where(full, (held - 1) % padded, -1)
    slots = n_dp * CAP
    own = jnp.arange(n_dp, dtype=jnp.int32)[:, None] * qd + item % qd
    own = jnp.where(full, own, -1).reshape(n_groups, slots)
    is_pos = (full & (item < qd)).reshape(n_groups, slots)
    member_no = jnp.arange(members, dtype=jnp.int32)
    onehot = (row.reshape(n_groups, slots)[:, :, None] == jnp.arange(block_rows)).astype(bf16)
    at_own = own[:, :, None] == member_no
    pick_pos = (at_own & is_pos[:, :, None]).astype(bf16)
    at_neg = at_own & ~is_pos[:, :, None]

    rows = jnp.einsum("gsp,pw->gsw", onehot, passages, preferred_element_type=f32).astype(bf16)
    pos_rows = jnp.einsum("gsc,gsw->gcw", pick_pos, rows, preferred_element_type=f32).astype(bf16)
    half = members // 2
    in_parts = [
        jnp.einsum("gqw,gcw->gqc", every_query, cols, preferred_element_type=f32)
        for cols in (pos_rows[:, :half], pos_rows[:, half:])
    ]
    slot_part = jnp.einsum("gsw,gqw->gsq", rows, every_query, preferred_element_type=f32)
    score = jnp.sum(jnp.where(at_neg, slot_part, 0.0), axis=2).reshape(n_groups, n_dp, CAP)
    neg_no = item_no[qd:items]
    neg_part = jnp.sum(
        jnp.where(item[:, :, :, None] == neg_no, score[:, :, :, None], 0.0), axis=2
    )
    neg_shape = (neg_count * qd // 128, 128)
    left, right, neg = scatter_scores([
        in_parts[0].reshape(lead + (qd, half)),
        in_parts[1].reshape(lead + (qd, half)),
        neg_part.reshape(lead + neg_shape),
    ])
    neg = neg.reshape(neg_count, qd).T
    logits = jnp.concatenate([left, right, neg], axis=1) * scale

    row_max = jnp.max(logits, axis=1, keepdims=True)
    exponent = jnp.exp(logits - row_max)
    denominator = jnp.sum(exponent, axis=1, keepdims=True)
    own_col = lax.axis_index("dp") * qd + jnp.arange(qd)
    target = (jnp.arange(members + neg_count)[None, :] == own_col[:, None]).astype(f32)
    losses = jnp.log(denominator[:, 0]) + row_max[:, 0] - jnp.sum(target * logits, axis=1)
    weights = (exponent / denominator - target).astype(bf16)

    left, right, neg = gather_weights([
        weights[:, :half],
        weights[:, half:members],
        weights[:, members:].T.astype(f32).reshape(neg_shape),
    ])
    neg_weights = neg.reshape(n_groups, n_dp, 1, neg_count * qd)
    slot_weight = jnp.sum(
        jnp.where(item[:, :, :, None] == neg_no, neg_weights, 0.0), axis=3
    ).reshape(n_groups, slots)
    spread = sum(
        jnp.einsum(
            "gsc,gqc->gsq", pick, w.reshape(n_groups, members, half), preferred_element_type=f32
        )
        for pick, w in ((pick_pos[..., :half], left), (pick_pos[..., half:], right))
    )
    spread = jnp.where(at_neg, slot_weight[:, :, None], spread).astype(bf16)
    share = n_t // len(GRAD_WALKS)
    group_share = share * n_c

    def query_part(first):
        part = jnp.einsum(
            "gsq,gsw->gqw", spread[first:first + group_share], rows[first:first + group_share],
            preferred_element_type=f32,
        ) * scale
        part = part.reshape((share, n_c * n_z * CORES, qd, width)).swapaxes(0, 1)
        return part.reshape(n_c, n_z, CORES, share, qd, width)

    grad_query = scatter_grads([query_part(n * group_share) for n in range(len(GRAD_WALKS))])
    slot_grads = jnp.einsum("gsq,gqw->gsw", spread, every_query, preferred_element_type=f32)
    slot_grads = (slot_grads * scale).astype(bf16)
    grad_pass = jnp.einsum("gsp,gsw->pw", onehot, slot_grads, preferred_element_type=f32)
    return (grad_query, losses, grad_pass)


def solution(mesh):
    in_specs = (
        P(("dp", "tensor", "corpus"), None),
        P(("dp", "corpus"), "tensor"),
        P(("dp", "tensor", "corpus")),
        P(("dp", "tensor", "corpus"), None),
    )
    out_specs = (
        P(("dp", "tensor", "corpus"), None),
        P(("dp", "tensor", "corpus")),
        P(("dp", "corpus"), "tensor"),
    )
    return jax.shard_map(body, mesh=mesh, in_specs=in_specs, out_specs=out_specs, check_vma=False)
```

time: 892 us -> 276 us (0.31)
  waiting for transfers between devices: 649 us -> 0 us
  Pallas kernels: 0 us -> 200 us
  blocking collectives: 140 us -> 0 us
  between operations: 14 us -> 0.89 us
  local copies, waits for them, and re-layouts: 28.8 us -> 17.6 us
    reduce_scatter x2 -> x0, waiting for transfers between devices: 539 us -> none  [the longest x1 394 us: scatter_scores(): lax.psum_scatter(part, ('dp', 'tensor', 'corpus'), scatter_dimension=0, t...]
    pallas_call x0 -> x4, Pallas kernels: none -> 200 us  [kernel_call(): pl.pallas_call(kernel, out_shape=outs, in_specs=[VMEM_SPEC] * len(inputs)...]
    all_gather x1 -> x0, blocking collectives: 130 us -> none  [gather_small(): lax.all_gather(values, ('dp', 'tensor', 'corpus'), axis=0, tiled=False)]
    all_gather x2 -> x0, waiting for transfers between devices: 109 us -> none  [the longest x1 109 us: gather_small(): lax.all_gather(values, ('dp', 'tensor', 'corpus'), axis=0, tiled=False)]
    all_to_all x1 -> x0, blocking collectives: 9.38 us -> none  [gather_queries(): lax.all_to_all(mine, 'tensor', split_axis=0, concat_axis=0, tiled=True)]
  transfers between devices with their start and end apart: 5 -> 0, of which waited for: 3 -> 0; matrix products, arithmetic and copies ran while one was open for 3% -> 0% of each run, Pallas kernels for 0% -> 0%
where the time goes in v2:
time: 276 us; the launch traced here: 271 us
  Pallas kernels  200 us (72%)
  matrix products  34.3 us (12%)
  local copies, waits for them, and re-layouts  17.6 us (6%)
  other arithmetic  17.5 us (6%)
    pallas_call x4, Pallas kernels, kernel_call(): pl.pallas_call(kernel, out_shape=outs, in_specs=[VMEM_SPEC] * len(inputs)...  200 us
    dot_general x1, matrix products, body(): jnp.einsum('gsp,gsw->pw', onehot, slot_grads, preferred_element_type=f32)  9.93 us

profile of v2, /device:TPU:1, one launch (start us, length us, event | category | flops | bytes accessed | tf_op | source)
XLA Modules:
  0.0 270.8 jit_solution(4326485138745542011)
XLA Ops:
  0.6 0.0 copy-start
  0.7 0.1 slice.36
  0.8 0.1 add.129
  0.8 0.1 add.130
  0.9 0.8 copy.31
  1.7 0.8 pad_add_fusion
  2.5 0.1 copy.32
  2.5 0.1 reshape.187
  2.6 0.6 pad.4.ids_in
  3.2 1.5 copy.54
  4.7 49.4 %shard_map.67 = (bf16[4,4,8,2,16,512]{5,4,3,2,1,0:T(8,128)(2,1)}, s32[4,4,8,2,1,640]{5,4,3,2,1,0:T(1,128)}) custom-call(bf16[4,16,512]{2,1,0:T(8,128)(2,1)} %bitcast.63, s32[1,640]{1,0:T(1,128)} %pad.4.ids_in), custom_call_target="tpu_custom_call" | custom-call | tf_op jit(solution)/shard_map/pallas_call | solution.py:230
  54.1 3.0 %reduce = s32[4,4,8,2,640]{4,3,2,1,0:T(2,128)S(1)} reduce(s32[4,4,8,2,1,640]{5,4,3,2,1,0:T(1,128)} %get-tuple-element.11, s32[]{:T(128)} %constant.71.clone.1), dimensions={4}, to_apply=%get-tuple-element.11.reduce_sub_computation | reduce | bytes 1310724 | tf_op jit(solution)/shard_map/pallas_call | solution.py:230
  57.1 0.5 reshape.188
  57.5 1.0 fusion.28
  58.5 0.3 fusion.35
  58.9 4.4 %select_reduce_fusion = s32[16,16,16]{2,1,0:T(8,128)S(1)} fusion(s32[16,16,640]{2,1,0:T(8,128)S(1)} %fusion.35, s32[16,16,640]{2,1,0:T(8,128)S(1)} %fusion.28), kind=kLoop, calls=%fused_computation.5 | loop fusion | flops 7860224 | bytes 1327104 | tf_op jit(solution)/shard_map/reduce_sum | solution.py:494
  63.3 0.1 ne.111
  63.4 0.1 add_remainder_fusion
  63.5 0.1 rem.89
  63.6 0.1 gt.31
  63.8 0.1 div.38
  63.9 1.7 fusion.7
  65.6 0.0 copy-done
  65.6 4.8 %fusion.11 = bf16[16,256,512]{2,1,0:T(8,128)(2,1)S(1)} fusion(s32[16,256]{1,0:T(8,128)S(1)} %get-tuple-element.30, bf16[1024,512]{1,0:T(8,128)(2,1)S(1)} %copy-done), kind=kOutput, calls=%fused_computation.19 | convolution fusion | flops 4301258752 | bytes 5259264 | tf_op jit(solution)/shard_map/gsp,pw->gsw/dot_general | solution.py:510
  70.4 0.0 copy-start.3
  70.4 2.0 copy-done.3
  72.4 0.0 copy-done.1
  72.4 1.5 select_reduce_fusion.1
  74.0 0.1 broadcast_in_dim.82
  74.1 2.5 fusion.2
  76.5 1.0 reshape.192.refs_2_
  77.5 3.6 %convolution_convert_fusion = bf16[16,256,512]{2,1,0:T(8,128)(2,1)S(1)} fusion(bf16[16,256,512]{2,1,0:T(8,128)(2,1)} %copy-done.3, s32[16,256]{1,0:T(8,128)S(1)} %get-tuple-element.29, pred[16,256]{1,0:T(8,128)(4,1)S(1)} %get-tuple-element.24), kind=kOutput, calls=%fused_computation.20 | convolution fusion | flops 1077936128 | bytes 8409088 | tf_op jit(solution)/shard_map/gsc,gsw->gcw/dot_general | solution.py:511
  81.1 0.0 copy-done.2
  81.1 2.6 fusion.14
  83.8 2.6 fusion.16
  86.3 43.9 %shard_map.68 = (f32[16,128]{1,0:T(8,128)}, f32[16,128]{1,0:T(8,128)}, f32[4,128]{1,0:T(4,128)}) custom-call(f32[4,4,8,2,16,128]{5,4,3,2,1,0:T(8,128)} %bitcast.58, f32[4,4,8,2,16,128]{5,4,3,2,1,0:T(8,128)} %bitcast.57, f32[4,4,8,2,4,128]{5,4,3,2,1,0:T(4,128)} %reshape.192.refs_2_), custom_call_target="tpu_custom_call" | custom-call | tf_op jit(solution)/shard_map/pallas_call | solution.py:230
  130.2 0.8 reshape.193
  131.0 0.1 copy.34
  131.1 0.8 fusion.60
  131.9 0.9 select_reduce_fusion.2
  132.8 0.8 subtract_convert_fusion
  133.6 0.5 add_subtract_fusion
  134.1 0.6 fusion.63
  134.7 0.1 copy.35
  134.8 0.7 reshape.204.refs_2_
  135.5 43.6 %shard_map.69 = (bf16[4,4,8,2,16,128]{5,4,3,2,1,0:T(8,128)(2,1)}, bf16[4,4,8,2,16,128]{5,4,3,2,1,0:T(8,128)(2,1)}, f32[4,4,8,2,4,128]{5,4,3,2,1,0:T(4,128)}) custom-call(bf16[16,128]{1,0:T(8,128)(2,1)} %get-tuple-element.32.refs_0_, bf16[16,128]{1,0:T(8,128)(2,1)} %get-tuple-element.31.refs_1_, f32[4,128]{1,0:T(4,128)} %reshape.204.refs_2_), custom_call_target="tpu_custom_call" | custom-call | tf_op jit(solution)/shard_map/pallas_call | solution.py:230
  179.1 0.0 copy-start.5
  179.1 1.3 broadcast_in_dim.85
  180.5 1.6 fusion.3
  182.1 0.0 copy-start.6
  182.1 0.1 broadcast_in_dim.87
  182.2 2.3 fusion.19
  184.5 0.0 copy-done.5
  184.5 0.0 copy-done.6
  184.5 2.8 %select_convert_fusion = bf16[16,256,256]{1,2,0:T(8,128)(2,1)} fusion(f32[16,256,256]{1,2,0:T(8,128)S(1)} %fusion.19, bf16[16,256,128]{2,1,0:T(8,128)(2,1)S(1)} %bitcast.71, bf16[16,256]{1,0:T(8,128)(2,1)S(1)} %broadcast_in_dim.87, s32[16,256]{1,0:T(8,128)S(1)} %get-tuple-element.29, pred[16,256,256]{1,2,0:T(32,128)(4,1)S(1)} %copy-done.5, ...), kind=kOutput, calls=%fused_computation.13 | convolution fusion | flops 272629760 | bytes 7892992 | tf_op jit(solution)/shard_map/gsc,gqc->gsq/dot_general | solution.py:550
  187.3 9.9 %fusion.24 = f32[1024,512]{1,0:T(8,128)} fusion(bf16[16,256,256]{1,2,0:T(8,128)(2,1)} %select_convert_fusion, bf16[16,256,512]{2,1,0:T(8,128)(2,1)} %bitcast.51, s32[16,256]{1,0:T(8,128)S(1)} %get-tuple-element.30), kind=kOutput, calls=%fused_computation.35 | convolution fusion | flops 5377097728 | bytes 8404992 | tf_op jit(solution)/shard_map/gsp,gsw->pw/dot_general | solution.py:570
  197.3 0.0 copy-done.7
  197.3 2.5 convolution_multiply_fusion
  199.7 0.4 copy-done.4
  200.1 0.7 convolution_multiply_fusion.1
  200.8 2.4 copy.40
  203.2 2.4 copy.41
  205.6 63.6 %shard_map.70 = f32[4,16,512]{2,1,0:T(8,128)} custom-call(f32[4,8,2,2,16,512]{5,4,3,2,1,0:T(8,128)} %bitcast.55, f32[4,8,2,2,16,512]{5,4,3,2,1,0:T(8,128)} %bitcast.56), custom_call_target="tpu_custom_call" | custom-call | tf_op jit(solution)/shard_map/pallas_call | solution.py:230
  269.2 1.6 copy.52
  (11 shorter events, 0.1 us)
Async XLA Ops:
  0.6 65.0 %copy-start = (bf16[1024,512]{1,0:T(8,128)(2,1)S(1)}, bf16[1024,512]{1,0:T(8,128)(2,1)}, u32[]{:S(2)}) copy-start(bf16[1024,512]{1,0:T(8,128)(2,1)} %param.5) | copy-start | bytes 3145732
  65.6 6.8 %copy-start.1 = (bf16[4,4,8,2,16,512]{5,4,3,2,1,0:T(8,128)(2,1)S(1)}, bf16[4,4,8,2,16,512]{5,4,3,2,1,0:T(8,128)(2,1)}, u32[]{:S(2)}) copy-start(bf16[4,4,8,2,16,512]{5,4,3,2,1,0:T(8,128)(2,1)} %get-tuple-element.12) | copy-start | bytes 12582916
  70.4 2.0 copy-start.3
  77.5 3.6 %copy-start.2 = (bf16[4,4,8,2,16,512]{5,4,3,2,1,0:T(8,128)(2,1)S(1)}, bf16[4,4,8,2,16,512]{5,4,3,2,1,0:T(8,128)(2,1)}, u32[]{:S(2)}) copy-start(bf16[4,4,8,2,16,512]{5,4,3,2,1,0:T(8,128)(2,1)} %get-tuple-element.12) | copy-start | bytes 12582916
  179.1 5.4 %copy-start.5 = (pred[16,256,256]{1,2,0:T(32,128)(4,1)S(1)}, pred[16,256,256]{1,2,0:T(32,128)(4,1)}, u32[]{:S(2)}) copy-start(pred[16,256,256]{1,2,0:T(32,128)(4,1)} %fusion.7) | copy-start | bytes 3145732
  182.1 2.4 copy-start.6
  187.3 9.9 %copy-start.7 = (bf16[16,256,256]{1,2,0:T(8,128)(2,1)S(1)}, bf16[16,256,256]{1,2,0:T(8,128)(2,1)}, u32[]{:S(2)}) copy-start(bf16[16,256,256]{1,2,0:T(8,128)(2,1)} %select_convert_fusion) | copy-start | bytes 6291460
  197.3 2.8 %copy-start.4 = (bf16[16,256,512]{2,1,0:T(8,128)(2,1)S(1)}, bf16[16,256,512]{2,1,0:T(8,128)(2,1)}, u32[]{:S(2)}) copy-start(bf16[16,256,512]{2,1,0:T(8,128)(2,1)} %copy-done.3) | copy-start | bytes 12582916

commit v3 on v2

v3 whole, which is shorter than its diff:
```python
import heapq
import math

import jax
import jax.numpy as jnp
from jax import lax
from jax.experimental import pallas as pl
from jax.experimental.pallas import tpu as pltpu
from jax.sharding import PartitionSpec as P

CAP = 16
VMEM_LIMIT = 62 * 1024 * 1024
CORES = 2


class Place:
    def __init__(self):
        dp = lax.axis_index("dp")
        self.size = {
            "z": lax.axis_size("dp") // CORES,
            "tensor": lax.axis_size("tensor"),
            "corpus": lax.axis_size("corpus"),
        }
        self.at = {
            "z": dp // CORES,
            "tensor": lax.axis_index("tensor"),
            "corpus": lax.axis_index("corpus"),
        }
        self.core = dp % CORES

    def along(self, axis, step):
        n = self.size[axis]
        return lax.rem(self.at[axis] + (step + n), n)

    def device(self, axis, step):
        if axis == "core":
            return {"dp": self.at["z"] * CORES + (1 - self.core)}
        spot = self.along(axis, step)
        if axis == "z":
            return {"dp": spot * CORES + self.core}
        return {axis: spot}

    def greet(self, peers):
        barrier = pltpu.get_barrier_semaphore()
        for axis, step in peers:
            pl.semaphore_signal(
                barrier, inc=1, device_id=self.device(axis, step),
                device_id_type=pl.DeviceIdType.MESH,
            )
        pl.semaphore_wait(barrier, len(peers))


LINK_RATE = 90e3
SWAP_RATE = 450e3


class Flow:
    def __init__(self, send_sem, recv_sem):
        self.send_sem, self.recv_sem = send_sem, recv_sem
        self.used = 0
        self.sent = []
        self.coming = []
        self.now = 0.0
        self.busy = {}

    def make(self, src, dst, device, number):
        return pltpu.make_async_remote_copy(
            src_ref=src, dst_ref=dst, send_sem=self.send_sem.at[number],
            recv_sem=self.recv_sem.at[number], device_id=device,
            device_id_type=pl.DeviceIdType.MESH,
        )

    def post(self, src, dst, device, landing, link, hops, then=None):
        number = self.used
        self.used += 1
        copy = self.make(src, dst, device, number)
        copy.start()
        self.sent.append(copy)
        size = math.prod(src.shape) * jnp.dtype(src.dtype).itemsize
        cost = size / SWAP_RATE if link == "core" else CORES * hops * size / LINK_RATE
        begin = max(self.now, self.busy.get(link, 0.0))
        self.busy[link] = begin + cost
        due = begin + cost + 0.8 + 0.7 * hops
        self.now += 0.01
        heapq.heappush(
            self.coming, (due, number, self.make(landing, landing, device, number), then)
        )

    def run(self):
        while self.coming:
            due, _, landing, then = heapq.heappop(self.coming)
            self.now = max(self.now, due)
            landing.wait_recv()
            if then is not None:
                then()
        for copy in self.sent:
            copy.wait_send()


def add_to(dst, first, others):
    if len(dst.shape) > 2 and math.prod(dst.shape) > 32 * 1024:
        def step(i, carry):
            add_to(dst.at[i], first.at[i], [o.at[i] for o in others])
            return carry
        lax.fori_loop(0, dst.shape[0], step, 0)
        return
    total = first[...].astype(jnp.float32)
    for o in others:
        total = total + o[...].astype(jnp.float32)
    dst[...] = total.astype(dst.dtype)


def direct_link(axis, step, n):
    way = 1 if step <= n // 2 else -1
    return (axis, way), min(step, n - step)


def ring_hops(n, flip=False):
    far, near = n // 2, n - 1 - n // 2
    return {1: near, -1: far} if flip else {1: far, -1: near}


def relay(flow, place, view, where, axis, way, hop, hops, have):
    at = dict(where, **{axis: place.along(axis, -way * hop)})
    coming = dict(where, **{axis: place.along(axis, -way * (hop + 1))})
    block = view(at, place.core)

    def then():
        if hop + 1 < hops:
            relay(flow, place, view, where, axis, way, hop + 1, hops, have)
        have(coming)

    flow.post(
        block, block, place.device(axis, way), view(coming, place.core), (axis, way), 1, then
    )


def spread(flow, place, view, where, axes, ring, have):
    for i, axis in enumerate(axes):
        rest = axes[i + 1:]

        def went(coming, rest=rest):
            spread(flow, place, view, coming, rest, ring, have)

        n = place.size[axis]
        if ring is not None and n > 4:
            hops = ring_hops(n, ring)
            for way in (1, -1):
                if hops[way]:
                    relay(flow, place, view, where, axis, way, 0, hops[way], went)
        else:
            block = view(where, place.core)
            for step in sorted(range(1, n), key=lambda s: min(s, n - s)):
                coming = dict(where, **{axis: place.along(axis, -step)})
                link, far = direct_link(axis, step, n)
                flow.post(
                    block, block, place.device(axis, step), view(coming, place.core), link, far,
                    lambda went=went, coming=coming: went(coming),
                )
    have(where)


def reduce_flow(flow, place, part, fold, dims, axes, boxes, holds, slims, out, done):
    def stage(k, held, dims):
        axis = axes[k]
        n = place.size[axis]
        spot = dims.index(axis)
        rest = dims[:spot] + dims[spot + 1:]
        box = boxes[k]
        last = k == len(axes) - 1
        target = out if last else holds[k]
        terms, left = [], [n]

        def place_of(step):
            return (slice(None),) * spot + (place.along(axis, step),)

        def finish():
            left[0] -= 1
            if left[0] == 0:
                add_to(target, held.at[place_of(0)], terms)
                if last:
                    done()
                else:
                    stage(k + 1, target, rest)

        def gate(step, then):
            piece = held.at[place_of(step)]
            into = slims[k].at[step - 1] if slims and step else piece
            if k > 0:
                if slims and step:
                    add_to(into, piece, [])
                then(into)
                return
            where = place_of(step) + (slice(None),) * (len(dims) - spot - 1)
            keep, give = part.at[where + (place.core,)], part.at[where + (1 - place.core,)]

            def folded():
                add_to(into, piece, [keep])
                then(into)

            flow.post(give, piece, place.device("core", 1), piece, "core", 0, folded)

        for step in sorted(range(1, n), key=lambda s: -min(s, n - s)):
            slot = box.at[step - 1]
            terms.append(slot)
            link, far = direct_link(axis, step, n)

            def send(src, slot=slot, step=step, link=link, far=far):
                flow.post(src, slot, place.device(axis, step), slot, link, far, finish)

            gate(step, send)
        gate(0, lambda src: finish())

    stage(0, fold, tuple(dims))


def reduce_scratch(sizes, dims, axes, chunk, narrow):
    def buffer(lead, kind=jnp.float32):
        return pltpu.VMEM(tuple(lead) + tuple(chunk), kind)

    kind = jnp.bfloat16 if narrow else jnp.float32
    left = list(dims)
    fold = buffer([sizes[d] for d in left])
    boxes, holds, slims = [], [], []
    for stage, axis in enumerate(axes):
        left.remove(axis)
        part = [sizes[d] for d in left]
        boxes.append(buffer([sizes[axis] - 1] + part, kind))
        if narrow:
            slims.append(buffer([sizes[axis] - 1] + part, kind))
        if stage < len(axes) - 1:
            holds.append(buffer(part))
    return [fold] + boxes + holds + slims


def split_scratch(refs, stages, narrow):
    refs = list(refs)
    fold, boxes, holds = refs[0], refs[1:1 + stages], refs[1 + stages:2 * stages]
    used = 3 * stages if narrow else 2 * stages
    return (fold, boxes, holds, refs[2 * stages:used]), refs[used:]


def reduce_copies(sizes, axes):
    return sizes[axes[0]] + sum(sizes[a] - 1 for a in axes)


def mesh_sizes():
    return {
        "z": lax.axis_size("dp") // CORES,
        "tensor": lax.axis_size("tensor"),
        "corpus": lax.axis_size("corpus"),
    }


def peers(place, axes):
    found = [("core", 1)]
    for axis in axes:
        found += [(axis, step) for step in range(1, place.size[axis])]
    return found


VMEM_SPEC = pl.BlockSpec(memory_space=pltpu.VMEM)


def kernel_call(kernel, outs, scratch, copies, number, inputs):
    return pl.pallas_call(
        kernel,
        out_shape=outs,
        in_specs=[VMEM_SPEC] * len(inputs),
        out_specs=[VMEM_SPEC] * len(outs),
        scratch_shapes=[
            pltpu.SemaphoreType.DMA((copies,)),
            pltpu.SemaphoreType.DMA((copies,)),
        ] + scratch,
        compiler_params=pltpu.CompilerParams(
            collective_id=number, has_side_effects=True, vmem_limit_bytes=VMEM_LIMIT
        ),
    )(*inputs)


def swapper(flow, place, view):
    def swap(where):
        block = view(where, place.core)
        landing = view(where, 1 - place.core)
        flow.post(block, block, place.device("core", 1), landing, "core", 0)
    return swap


def query_kernel(q_in, ids_in, q_out, ids_out, send_sem, recv_sem, own_sem):
    place = Place()
    flow = Flow(send_sem, recv_sem)
    n_t = place.size["tensor"]
    t, c, z, core = place.at["tensor"], place.at["corpus"], place.at["z"], place.core
    place.greet(peers(place, ("z", "corpus", "tensor")))
    keep = [
        pltpu.make_async_copy(q_in.at[t], q_out.at[t, c, z, core], own_sem.at[0]),
        pltpu.make_async_copy(ids_in, ids_out.at[t, c, z, core], own_sem.at[1]),
    ]
    for copy in keep:
        copy.start()
    half = n_t // 2

    def of(ref, part):
        return lambda where, k: ref.at[part, where["corpus"], where["z"], k]

    left = [2 * (n_t - 1)]

    def begin():
        left[0] -= 1
        if left[0]:
            return
        for copy in keep:
            copy.wait()
        for ref, part, axes, ring in (
            (q_out, slice(half, n_t), ("z", "corpus"), True),
            (q_out, slice(0, half), ("corpus", "z"), False),
            (ids_out, slice(0, n_t), ("corpus", "z"), True),
        ):
            view = of(ref, part)
            spread(
                flow, place, view, {"corpus": c, "z": z}, axes, ring, swapper(flow, place, view)
            )

    for step in range(1, n_t):
        peer, source = place.along("tensor", step), place.along("tensor", -step)
        link, far = direct_link("tensor", step, n_t)
        device = place.device("tensor", step)
        flow.post(
            q_in.at[peer], q_out.at[t, c, z, core], device, q_out.at[source, c, z, core],
            link, far, begin,
        )
        flow.post(
            ids_in, ids_out.at[t, c, z, core], device, ids_out.at[source, c, z, core],
            link, far, begin,
        )
    flow.run()


def gather_queries(queries, ids):
    sizes = mesh_sizes()
    n_t, n_c, n_z = sizes["tensor"], sizes["corpus"], sizes["z"]
    qd, feat = queries.shape
    width = feat // n_t
    mine = queries.reshape(qd, n_t, width).swapaxes(0, 1)
    lead = (n_t, n_c, n_z, CORES)
    count = ids.shape[1]
    copies = 2 * (n_t - 1) + 3 * (2 * n_c * n_z - 1)
    every_query, every_id = kernel_call(
        query_kernel,
        [
            jax.ShapeDtypeStruct(lead + (qd, width), queries.dtype),
            jax.ShapeDtypeStruct(lead + (1, count), ids.dtype),
        ],
        [pltpu.SemaphoreType.DMA((2,))], copies, 0, (mine, ids),
    )
    groups, members = n_t * n_c, n_z * CORES
    return (
        every_query.reshape(groups, members * qd, width),
        every_id.reshape(groups, members, count),
    )


def weight_kernel(*refs):
    parts = 3
    ins, outs = refs[:parts], refs[parts:2 * parts]
    send_sem, recv_sem, own_sem = refs[2 * parts:]
    place = Place()
    flow = Flow(send_sem, recv_sem)
    n_t, n_c, n_z = (place.size[a] for a in ("tensor", "corpus", "z"))
    t, c, z, core = place.at["tensor"], place.at["corpus"], place.at["z"], place.core
    plane = [(a, b) for a in range(n_t) for b in range(n_c) if a or b]
    plane.sort(key=lambda o: -(min(o[0], n_t - o[0]) + min(o[1], n_c - o[1])))

    def over(a, b):
        return {"tensor": place.along("tensor", a), "corpus": place.along("corpus", b)}

    barrier = pltpu.get_barrier_semaphore()
    others = [place.device("core", 1)] + [place.device("z", w) for w in range(1, n_z)]
    others += [over(a, b) for a, b in plane]
    for device in others:
        pl.semaphore_signal(
            barrier, inc=1, device_id=device, device_id_type=pl.DeviceIdType.MESH
        )
    pl.semaphore_wait(barrier, len(others))
    keep = [
        pltpu.make_async_copy(i, o.at[t, c, z, core], own_sem.at[n])
        for n, (i, o) in enumerate(zip(ins, outs))
    ]
    for copy in keep:
        copy.start()
    for copy in keep:
        copy.wait()
    here = {"tensor": t, "corpus": c, "z": z}
    every = {"tensor": slice(None), "corpus": slice(None), "z": slice(None)}

    def of(ref):
        return lambda where, k: ref.at[where["tensor"], where["corpus"], where["z"], k]

    def to_plane(view, where, then):
        block = view(where, core)
        for a, b in plane:
            coming = dict(where, **over(-a, -b))
            far = min(a, n_t - a) + min(b, n_c - b)
            link = direct_link("tensor", a, n_t)[0] if a else direct_link("corpus", b, n_c)[0]
            flow.post(
                block, block, over(a, b), view(coming, core), link, far,
                lambda coming=coming: then(coming),
            )

    def around(view, where, have, flip):
        hops = ring_hops(n_z, flip)
        for way in (1, -1):
            if hops[way]:
                relay(flow, place, view, where, "z", way, 0, hops[way], have)

    for ref in outs[1:]:
        view = of(ref)
        swap = swapper(flow, place, view)
        left = [len(plane)]

        def landed(coming, view=view, swap=swap, left=left):
            left[0] -= 1
            if left[0] == 0:
                whole = dict(every, z=z)
                around(view, whole, swap, False)
                swap(whole)

        to_plane(view, here, landed)

    view = of(outs[0])
    swap = swapper(flow, place, view)
    count = [n_z - 1]

    def stacked():
        count[0] -= 1
        if count[0] == 0:
            column = dict(here, z=slice(None))
            to_plane(view, column, swap)
            swap(column)

    for step in range(1, n_z):
        coming = dict(here, z=place.along("z", -step))
        link, far = direct_link("z", step, n_z)
        block = view(here, core)
        flow.post(block, block, place.device("z", step), view(coming, core), link, far, stacked)
    flow.run()


def gather_weights(parts):
    sizes = mesh_sizes()
    n_t, n_c, n_z = sizes["tensor"], sizes["corpus"], sizes["z"]
    lead = (n_t, n_c, n_z, CORES)
    flat = n_t * n_c
    copies = 3 * (flat - 1 + n_z - 1) + 2 * n_z + flat
    return kernel_call(
        weight_kernel,
        [jax.ShapeDtypeStruct(lead + p.shape, p.dtype) for p in parts],
        [pltpu.SemaphoreType.DMA((len(parts),))], copies, 1, tuple(parts),
    )


SCORE_DIMS = ("tensor", "corpus", "z")
SCORE_WALKS = (
    ("tensor", "corpus", "z"),
    ("corpus", "tensor", "z"),
    ("z", "corpus", "tensor"),
)


def score_kernel(*refs):
    parts = len(SCORE_WALKS)
    ins, outs = refs[:parts], refs[parts:2 * parts]
    send_sem, recv_sem = refs[2 * parts:2 * parts + 2]
    scratch = refs[2 * parts + 2:]
    place = Place()
    flow = Flow(send_sem, recv_sem)
    place.greet(peers(place, SCORE_DIMS))
    for n, axes in enumerate(SCORE_WALKS):
        (fold, boxes, holds, slims), scratch = split_scratch(scratch, len(axes), False)
        reduce_flow(
            flow, place, ins[n], fold, SCORE_DIMS, axes, boxes, holds, slims, outs[n],
            lambda: None,
        )
    flow.run()


def scatter_scores(parts):
    sizes = mesh_sizes()
    scratch = []
    chunks = [p.shape[4:] for p in parts]
    for chunk, axes in zip(chunks, SCORE_WALKS):
        scratch += reduce_scratch(sizes, SCORE_DIMS, axes, chunk, False)
    copies = sum(reduce_copies(sizes, axes) for axes in SCORE_WALKS)
    return kernel_call(
        score_kernel, [jax.ShapeDtypeStruct(c, jnp.float32) for c in chunks],
        scratch, copies, 2, tuple(parts),
    )


GRAD_DIMS = ("corpus", "z")


def grad_walks(n_t):
    first = max(1, 3 * n_t // 4)
    return [("corpus", "z")] * first + [("z", "corpus")] * (n_t - first)


def grad_kernel(part, out, send_sem, recv_sem, own_sem, total, *scratch):
    place = Place()
    flow = Flow(send_sem, recv_sem)
    n_t, t = place.size["tensor"], place.at["tensor"]
    place.greet(peers(place, ("corpus", "z", "tensor")))
    left = [n_t]
    keep = pltpu.make_async_copy(total.at[t], out.at[t], own_sem.at[0])

    def done():
        left[0] -= 1
        if left[0]:
            return
        keep.start()
        for step in range(1, n_t):
            peer, source = place.along("tensor", step), place.along("tensor", -step)
            link, far = direct_link("tensor", step, n_t)
            flow.post(
                total.at[peer], out.at[t], place.device("tensor", step), out.at[source], link, far
            )

    walks = grad_walks(n_t)
    order = sorted(range(n_t), key=lambda n: walks[n] != walks[-1])
    slots = []
    for axes in walks:
        held, scratch = split_scratch(scratch, len(axes), True)
        slots.append(held)
    for n in order:
        fold, boxes, holds, slims = slots[n]
        reduce_flow(
            flow, place, part.at[n], fold, GRAD_DIMS, walks[n], boxes, holds, slims,
            total.at[n], done,
        )
    flow.run()
    keep.wait()


def scatter_grads(part):
    sizes = mesh_sizes()
    qd, width = part.shape[4:]
    n_t = sizes["tensor"]
    scratch = [pltpu.SemaphoreType.DMA((1,)), pltpu.VMEM((n_t, qd, width), jnp.float32)]
    copies = n_t - 1
    for axes in grad_walks(n_t):
        scratch += reduce_scratch(sizes, GRAD_DIMS, axes, (qd, width), True)
        copies += reduce_copies(sizes, axes)
    (mine,) = kernel_call(
        grad_kernel, [jax.ShapeDtypeStruct((n_t, qd, width), jnp.float32)],
        scratch, copies, 3, (part,),
    )
    return mine.swapaxes(0, 1).reshape(qd, n_t * width)


def body(queries, passages, pos_ids, neg_ids):
    sizes = mesh_sizes()
    n_t, n_c, n_z = sizes["tensor"], sizes["corpus"], sizes["z"]
    n_dp = n_z * CORES
    qd, feat = queries.shape
    block_rows, width = passages.shape
    neg_count = neg_ids.shape[1]
    n_groups = n_t * n_c
    members = n_dp * qd
    items = (neg_count + 1) * qd
    padded = -(-(items + 1) // 128) * 128
    scale = feat ** (-0.5)
    f32, bf16 = jnp.float32, jnp.bfloat16
    block = lax.axis_index("dp") * n_c + lax.axis_index("corpus")
    lead = (n_t, n_c, n_z, CORES)

    ids = jnp.concatenate([pos_ids[None, :], neg_ids.T], axis=0).reshape(1, items)
    ids = jnp.pad(ids, ((0, 0), (0, padded - items)), constant_values=-1)
    every_query, every_id = gather_queries(queries, ids)

    item_no = jnp.arange(padded, dtype=jnp.int32)
    match = every_id // block_rows == block
    before = (item_no[:, None] < item_no[None, :]).astype(bf16)
    rank = jnp.einsum("gdj,jk->gdk", match.astype(bf16), before, preferred_element_type=f32)
    rank = jnp.where(match, rank.astype(jnp.int32), -1)
    packed = (every_id % block_rows) * padded + item_no + 1
    slot_no = jnp.arange(CAP, dtype=jnp.int32)
    held = jnp.sum(
        jnp.where(rank[:, :, None, :] == slot_no[:, None], packed[:, :, None, :], 0), axis=3
    )
    full = held > 0
    row = jnp.where(full, (held - 1) // padded, -1)
    item = jnp.where(full, (held - 1) % padded, -1)
    slots = n_dp * CAP
    own = jnp.arange(n_dp, dtype=jnp.int32)[:, None] * qd + item % qd
    own = jnp.where(full, own, -1).reshape(n_groups, slots)
    is_pos = (full & (item < qd)).reshape(n_groups, slots)
    member_no = jnp.arange(members, dtype=jnp.int32)
    onehot = (row.reshape(n_groups, slots)[:, :, None] == jnp.arange(block_rows)).astype(bf16)
    at_own = own[:, :, None] == member_no
    pick_pos = (at_own & is_pos[:, :, None]).astype(bf16)
    at_neg = at_own & ~is_pos[:, :, None]

    rows = jnp.einsum("gsp,pw->gsw", onehot, passages, preferred_element_type=f32).astype(bf16)
    pos_rows = jnp.einsum("gsc,gsw->gcw", pick_pos, rows, preferred_element_type=f32).astype(bf16)
    half = members // 2
    in_parts = [
        jnp.einsum("gqw,gcw->gqc", every_query, cols, preferred_element_type=f32)
        for cols in (pos_rows[:, :half], pos_rows[:, half:])
    ]
    slot_part = jnp.einsum("gsw,gqw->gsq", rows, every_query, preferred_element_type=f32)
    score = jnp.sum(jnp.where(at_neg, slot_part, 0.0), axis=2).reshape(n_groups, n_dp, CAP)
    neg_no = item_no[qd:items]
    neg_part = jnp.sum(
        jnp.where(item[:, :, :, None] == neg_no, score[:, :, :, None], 0.0), axis=2
    )
    neg_shape = (neg_count * qd // 128, 128)
    left, right, neg = scatter_scores([
        in_parts[0].reshape(lead + (qd, half)),
        in_parts[1].reshape(lead + (qd, half)),
        neg_part.reshape(lead + neg_shape),
    ])
    neg = neg.reshape(neg_count, qd).T
    logits = jnp.concatenate([left, right, neg], axis=1) * scale

    row_max = jnp.max(logits, axis=1, keepdims=True)
    exponent = jnp.exp(logits - row_max)
    denominator = jnp.sum(exponent, axis=1, keepdims=True)
    own_col = lax.axis_index("dp") * qd + jnp.arange(qd)
    target = (jnp.arange(members + neg_count)[None, :] == own_col[:, None]).astype(f32)
    losses = jnp.log(denominator[:, 0]) + row_max[:, 0] - jnp.sum(target * logits, axis=1)
    weights = (exponent / denominator - target).astype(bf16)

    left, right, neg = gather_weights([
        weights[:, :half],
        weights[:, half:members],
        weights[:, members:].T.astype(f32).reshape(neg_shape),
    ])
    neg_weights = neg.reshape(n_groups, n_dp, 1, neg_count * qd)
    slot_weight = jnp.sum(
        jnp.where(item[:, :, :, None] == neg_no, neg_weights, 0.0), axis=3
    ).reshape(n_groups, slots)
    mixed = sum(
        jnp.einsum(
            "gsc,gqc->gsq", pick, w.reshape(n_groups, members, half), preferred_element_type=f32
        )
        for pick, w in ((pick_pos[..., :half], left), (pick_pos[..., half:], right))
    )
    mixed = jnp.where(at_neg, slot_weight[:, :, None], mixed).astype(bf16)
    query_part = jnp.einsum("gsq,gsw->gqw", mixed, rows, preferred_element_type=f32) * scale
    grad_query = scatter_grads(query_part.reshape(lead + (qd, width)))
    slot_grads = jnp.einsum("gsq,gqw->gsw", mixed, every_query, preferred_element_type=f32)
    slot_grads = (slot_grads * scale).astype(bf16)
    grad_pass = jnp.einsum("gsp,gsw->pw", onehot, slot_grads, preferred_element_type=f32)
    return (grad_query, losses, grad_pass)


def solution(mesh):
    in_specs = (
        P(("dp", "tensor", "corpus"), None),
        P(("dp", "corpus"), "tensor"),
        P(("dp", "tensor", "corpus")),
        P(("dp", "tensor", "corpus"), None),
    )
    out_specs = (
        P(("dp", "tensor", "corpus"), None),
        P(("dp", "tensor", "corpus")),
        P(("dp", "corpus"), "tensor"),
    )
    return jax.shard_map(body, mesh=mesh, in_specs=in_specs, out_specs=out_specs, check_vma=False)
```

time: 276 us -> 233 us (0.84); the launches traced: 271 us -> 231 us
  Pallas kernels: 200 us -> 164 us
  local copies, waits for them, and re-layouts: 17.6 us -> 12.3 us
    pallas_call x4, Pallas kernels: 200 us -> 164 us  [kernel_call(): pl.pallas_call(kernel, out_shape=outs, in_specs=[VMEM_SPEC] * len(inputs)...]
    reshape x2 -> x0, local copies, waits for them, and re-layouts: 4.81 us -> none  [query_part(): part = part.reshape((share, n_c * n_z * CORES, qd, width)).swapaxes(0, 1)]
    dot_general x2 -> x1, matrix products: 3.17 us -> 6.66 us  [body(): jnp.einsum('gsq,gsw->gqw', mixed, rows, preferred_element_type=f32) * scale]
where the time goes in v3:
time: 233 us; the launch traced here: 231 us
  Pallas kernels  164 us (70%)
  matrix products  37 us (16%)
  other arithmetic  16.5 us (7%)
  local copies, waits for them, and re-layouts  12.3 us (5%)
    pallas_call x4, Pallas kernels, kernel_call(): pl.pallas_call(kernel, out_shape=outs, in_specs=[VMEM_SPEC] * len(inputs)...  164 us
    dot_general x1, matrix products, body(): jnp.einsum('gsp,gsw->pw', onehot, slot_grads, preferred_element_type=f32)  9.15 us
    dot_general x1, matrix products, body(): jnp.einsum('gsq,gsw->gqw', mixed, rows, preferred_element_type=f32) * scale  6.66 us
    dot_general x2, matrix products, body(): jnp.einsum('gqw,gcw->gqc', every_query, cols, preferred_element_type=f32)  5.15 us
    dot_general x1, matrix products, body(): jnp.einsum('gsp,pw->gsw', onehot, passages, preferred_element_type=f32)  4.99 us
    dot_general x2, matrix products, body(): jnp.einsum('gsc,gqc->gsq', pick, w.reshape(n_groups, members, half), pref...  4.89 us

profile of v3, /device:TPU:1, one launch (start us, length us, event | category | flops | bytes accessed | tf_op | source)
XLA Modules:
  0.0 230.6 jit_solution(17921111928660266278)
XLA Ops:
  0.6 0.0 copy-start
  0.7 1.6 copy.48
  2.2 0.7 copy.27
  2.9 0.8 pad_add_fusion
  3.7 0.1 copy.28
  3.8 0.1 reshape.178
  3.9 0.6 pad.4.ids_in
  4.5 48.9 %shard_map.67 = (bf16[4,4,8,2,16,512]{5,4,3,2,1,0:T(8,128)(2,1)}, s32[4,4,8,2,1,640]{5,4,3,2,1,0:T(1,128)}) custom-call(bf16[4,16,512]{2,1,0:T(8,128)(2,1)} %bitcast.53, s32[1,640]{1,0:T(1,128)} %pad.4.ids_in), custom_call_target="tpu_custom_call" | custom-call | tf_op jit(solution)/shard_map/pallas_call | solution.py:266
  53.4 3.0 %reduce = s32[4,4,8,2,640]{4,3,2,1,0:T(2,128)S(1)} reduce(s32[4,4,8,2,1,640]{5,4,3,2,1,0:T(1,128)} %get-tuple-element.11, s32[]{:T(128)} %constant.70.clone.1), dimensions={4}, to_apply=%get-tuple-element.11.reduce_sub_computation | reduce | bytes 1310724 | tf_op jit(solution)/shard_map/pallas_call | solution.py:266
  56.4 0.5 reshape.179
  56.9 1.0 fusion.26
  57.9 0.3 fusion.33
  58.2 4.4 %select_reduce_fusion = s32[16,16,16]{2,1,0:T(8,128)S(1)} fusion(s32[16,16,640]{2,1,0:T(8,128)S(1)} %fusion.33, s32[16,16,640]{2,1,0:T(8,128)S(1)} %fusion.26), kind=kLoop, calls=%fused_computation.5 | loop fusion | flops 7860224 | bytes 1327104 | tf_op jit(solution)/shard_map/reduce_sum | solution.py:587
  62.6 0.1 add_remainder_fusion
  62.7 0.1 rem.89
  62.8 0.1 gt.31
  63.0 0.1 div.38
  63.1 0.1 ne.111
  63.2 0.1 add.129
  63.3 0.1 add.130
  63.4 0.0 copy-done
  63.4 0.0 copy-start.2
  63.4 5.0 %fusion.11 = bf16[16,256,512]{2,1,0:T(8,128)(2,1)S(1)} fusion(s32[16,256]{1,0:T(8,128)S(1)} %get-tuple-element.30, bf16[1024,512]{1,0:T(8,128)(2,1)S(1)} %copy-done), kind=kOutput, calls=%fused_computation.20 | convolution fusion | flops 4301258752 | bytes 5259264 | tf_op jit(solution)/shard_map/gsp,pw->gsw/dot_general | solution.py:603
  68.4 0.0 copy-start.1
  68.5 1.9 copy-done.1
  70.4 0.0 copy-done.2
  70.4 1.5 select_reduce_fusion.1
  72.0 0.1 broadcast_in_dim.82
  72.1 0.1 slice.24
  72.2 2.5 %fusion.2 = f32[16,16,512]{2,1,0:T(8,128)S(1)} fusion(f32[16,16,16]{2,1,0:T(8,128)S(1)} %broadcast_in_dim.82, s32[512]{0:T(512)S(1)} %slice.24, s32[16,16,16]{2,1,0:T(8,128)S(1)} %get-tuple-element.27), kind=kLoop, calls=%fused_computation.7 | loop fusion | flops 6160384 | bytes 559104 | tf_op jit(solution)/shard_map/reduce_sum | solution.py:613
  74.6 1.0 reshape.183.refs_2_
  75.6 0.0 copy-start.3
  75.6 3.6 %convolution_convert_fusion = bf16[16,256,512]{2,1,0:T(8,128)(2,1)S(1)} fusion(bf16[16,256,512]{2,1,0:T(8,128)(2,1)} %copy-done.1, s32[16,256]{1,0:T(8,128)S(1)} %get-tuple-element.29, pred[16,256]{1,0:T(8,128)(4,1)S(1)} %get-tuple-element.24), kind=kOutput, calls=%fused_computation.21 | convolution fusion | flops 1077936128 | bytes 8409088 | tf_op jit(solution)/shard_map/gsc,gsw->gcw/dot_general | solution.py:604
  79.2 0.0 copy-done.3
  79.2 2.6 %fusion.12 = f32[16,256,128]{2,1,0:T(8,128)} fusion(bf16[16,256,512]{2,1,0:T(8,128)(2,1)S(1)} %bitcast.47, bf16[16,256,512]{2,1,0:T(8,128)(2,1)S(1)} %convolution_convert_fusion), kind=kOutput, calls=%fused_computation.22 | convolution fusion | flops 536870912 | bytes 8388608 | tf_op jit(solution)/shard_map/gqw,gcw->gqc/dot_general | solution.py:607
  81.8 2.6 %fusion.14 = f32[16,256,128]{2,1,0:T(8,128)} fusion(bf16[16,256,512]{2,1,0:T(8,128)(2,1)S(1)} %bitcast.48, bf16[16,256,512]{2,1,0:T(8,128)(2,1)S(1)} %convolution_convert_fusion), kind=kOutput, calls=%fused_computation.24 | convolution fusion | flops 536870912 | bytes 8388608 | tf_op jit(solution)/shard_map/gqw,gcw->gqc/dot_general | solution.py:607
  84.4 34.1 %shard_map.68 = (f32[16,128]{1,0:T(8,128)}, f32[16,128]{1,0:T(8,128)}, f32[4,128]{1,0:T(4,128)}) custom-call(f32[4,4,8,2,16,128]{5,4,3,2,1,0:T(8,128)} %bitcast.50, f32[4,4,8,2,16,128]{5,4,3,2,1,0:T(8,128)} %bitcast.49, f32[4,4,8,2,4,128]{5,4,3,2,1,0:T(4,128)} %reshape.183.refs_2_), custom_call_target="tpu_custom_call" | custom-call | tf_op jit(solution)/shard_map/pallas_call | solution.py:266
  118.5 0.7 reshape.184
  119.3 0.1 copy.30
  119.3 0.8 fusion.58
  120.2 0.9 select_reduce_fusion.2
  121.1 0.8 subtract_convert_fusion
  121.9 0.1 copy.31
  122.0 0.7 reshape.192.refs_2_
  122.7 0.6 fusion.61
  123.3 35.9 %shard_map.69 = (bf16[4,4,8,2,16,128]{5,4,3,2,1,0:T(8,128)(2,1)}, bf16[4,4,8,2,16,128]{5,4,3,2,1,0:T(8,128)(2,1)}, f32[4,4,8,2,4,128]{5,4,3,2,1,0:T(4,128)}) custom-call(bf16[16,128]{1,0:T(8,128)(2,1)} %get-tuple-element.32.refs_0_, bf16[16,128]{1,0:T(8,128)(2,1)} %get-tuple-element.31.refs_1_, f32[4,128]{1,0:T(4,128)} %reshape.192.refs_2_), custom_call_target="tpu_custom_call" | custom-call | tf_op jit(solution)/shard_map/pallas_call | solution.py:266
  159.2 1.3 broadcast_in_dim.85
  160.4 1.6 fusion.3
  162.1 0.1 broadcast_in_dim.87
  162.2 0.7 fusion.7
  162.9 2.1 fusion.17
  165.0 2.8 %select_convert_fusion = bf16[16,256,256]{1,2,0:T(8,128)(2,1)S(1)} fusion(f32[16,256,256]{1,2,0:T(8,128)S(1)} %fusion.17, bf16[16,256,128]{2,1,0:T(8,128)(2,1)} %bitcast.61, bf16[16,256]{1,0:T(8,128)(2,1)S(1)} %broadcast_in_dim.87, s32[16,256]{1,0:T(8,128)S(1)} %get-tuple-element.29, pred[16,256,256]{1,2,0:T(32,128)(4,1)S(1)} %fusion.7, ...), kind=kOutput, calls=%fused_computation.14 | convolution fusion | flops 272629760 | bytes 7892992 | tf_op jit(solution)/shard_map/gsc,gqc->gsq/dot_general | solution.py:643
  167.8 9.2 %fusion.22 = f32[1024,512]{1,0:T(8,128)} fusion(bf16[16,256,256]{1,2,0:T(8,128)(2,1)S(1)} %select_convert_fusion, bf16[16,256,512]{2,1,0:T(8,128)(2,1)} %bitcast.45, s32[16,256]{1,0:T(8,128)S(1)} %get-tuple-element.30), kind=kOutput, calls=%fused_computation.32 | convolution fusion | flops 5377097728 | bytes 8404992 | tf_op jit(solution)/shard_map/gsp,gsw->pw/dot_general | solution.py:653
  176.9 0.5 add_subtract_fusion
  177.5 6.7 %broadcast_multiply_fusion = f32[16,256,512]{2,1,0:T(8,128)} fusion(bf16[16,256,256]{1,2,0:T(8,128)(2,1)S(1)} %select_convert_fusion, bf16[16,256,512]{2,1,0:T(8,128)(2,1)} %copy-done.1), kind=kOutput, calls=%fused_computation.13 | convolution fusion | flops 1075838976 | bytes 14680064 | tf_op jit(solution)/shard_map/gsq,gsw->gqw/dot_general | solution.py:649
  184.1 44.9 %shard_map.70 = f32[4,16,512]{2,1,0:T(8,128)} custom-call(f32[4,4,8,2,16,512]{5,4,3,2,1,0:T(8,128)} %bitcast.44), custom_call_target="tpu_custom_call" | custom-call | tf_op jit(solution)/shard_map/pallas_call | solution.py:266
  229.0 1.6 copy.46
  (7 shorter events, 0.1 us)
Async XLA Ops:
  0.6 62.8 %copy-start = (bf16[1024,512]{1,0:T(8,128)(2,1)S(1)}, bf16[1024,512]{1,0:T(8,128)(2,1)}, u32[]{:S(2)}) copy-start(bf16[1024,512]{1,0:T(8,128)(2,1)} %param.5) | copy-start | bytes 3145732
  63.4 7.0 %copy-start.2 = (bf16[4,4,8,2,16,512]{5,4,3,2,1,0:T(8,128)(2,1)S(1)}, bf16[4,4,8,2,16,512]{5,4,3,2,1,0:T(8,128)(2,1)}, u32[]{:S(2)}) copy-start(bf16[4,4,8,2,16,512]{5,4,3,2,1,0:T(8,128)(2,1)} %get-tuple-element.12) | copy-start | bytes 12582916
  68.4 2.0 copy-start.1
  75.6 3.6 %copy-start.3 = (bf16[4,4,8,2,16,512]{5,4,3,2,1,0:T(8,128)(2,1)S(1)}, bf16[4,4,8,2,16,512]{5,4,3,2,1,0:T(8,128)(2,1)}, u32[]{:S(2)}) copy-start(bf16[4,4,8,2,16,512]{5,4,3,2,1,0:T(8,128)(2,1)} %get-tuple-element.12) | copy-start | bytes 12582916
